TPU v7x, 32 devices: a whole 2x2x4 slice. The times are simulated.
32 devices in a mesh: grp: 2 (over core), tile: 16 (over z, y, x).
Axes of the slice: x: 2, y: 2, z: 4, core: 2. Of those that a mesh axis runs over, the one named last changes fastest.
Arguments:
- basis: bfloat16 [32, 5, 64, 16, 128], P(None, None, 'tile'), may hold values from -18 to 18
- snapshots: bfloat16 [2, 4, 64, 16, 128], P('grp', None, 'tile'), may hold values from -1.5 to 1.5
- coupling: float32 [5, 5], replicated, may hold values from -2.5 to 2.5
Outputs:
- new_vector: float32 [2, 5, 64, 16, 128], P('grp', None, 'tile')
- coefficients: float32 [2, 32], P('grp')
- norms: float32 [2], P('grp')
All inputs are finite; a program needn't handle non-finite values.
Results may differ from a plain program's by a relative error of at most 0.0003.
Values may be sent and summed in bfloat16 or wider, within the bound.
A program may use at most 64 MiB of HBM per device.

v0:
```python
import functools

import jax
import jax.numpy as jnp
from jax import lax
from jax.experimental import pallas as pl
from jax.experimental.pallas import tpu as pltpu
from jax.sharding import PartitionSpec as P

viscosity = 0.5
time_step = 0.3
cancel_limit = 0.01
f32 = jnp.float32
bf16 = jnp.bfloat16
MESH = pl.DeviceIdType.MESH
HIGHEST = lax.Precision.HIGHEST


def spans(slab, rim):
    found = {}
    reach = -(-rim // slab)
    for d in range(1, reach + 1):
        width = min(slab, rim - (d - 1) * slab)
        found[-d] = (slab - width, slab)
        found[d] = (0, width)
    return found


def gram_blocks(krylov, lanes):
    blocks = max(lanes // krylov, 1)
    return (blocks, krylov // blocks) if krylov % (8 * blocks) == 0 else (1, krylov)


def stage(src, old, dst, snap, step, coupling, lo, hi, keep, gain):
    rows, lanes = src.shape[2], src.shape[3]
    row = lax.broadcasted_iota(jnp.int32, (rows, lanes), 0)
    first = row == 0
    last = row == rows - 1
    step_gain = time_step * gain
    mix = [[coupling[k, j] for j in range(5)] for k in range(5)]

    def body(i, carry):
        p = lo + i
        base = [snap[step, n, p].astype(f32) for n in range(4)]
        half = [(0.5 * step_gain) * base[n] for n in range(3)]
        edge = viscosity * step_gain
        x_up, x_low = edge - half[0], edge + half[0]
        y_up = jnp.where(last, 0.0, edge - half[1])
        y_low = jnp.where(first, 0.0, edge + half[1])
        z_up, z_low = edge - half[2], edge + half[2]
        pull = step_gain * base[3]
        center = [src[k, p] for k in range(5)]
        own = gain - 6.0 * viscosity * step_gain
        for k in range(5):
            q = center[k]
            coupled = mix[k][0] * center[0]
            for j in range(1, 5):
                coupled = coupled + mix[k][j] * center[j]
            total = own * q - pull * coupled
            total = total + (x_up * src[k, p + 1] + x_low * src[k, p - 1])
            total = total + (y_up * pltpu.roll(q, rows - 1, 0) + y_low * pltpu.roll(q, 1, 0))
            total = total + (z_up * pltpu.roll(q, lanes - 1, 1) + z_low * pltpu.roll(q, 1, 1))
            if keep:
                total = total + keep * old[k, p]
            dst[k, p] = total
        return carry

    lax.fori_loop(0, hi - lo, body, 0, unroll=4)


def kernel(
    groups, tiles, coupling, basis, snapshots,
    left, coef_out, square_out, margin_out,
    held, start, snap, state, one, two, cross, rows_k, spread,
    gram_send, gram_all, coef_send, coef_all,
    load_sem, start_send, start_recv, snap_send, snap_recv,
    gram_ssem, gram_rsem, coef_ssem, coef_rsem,
):
    g = lax.axis_index("grp")
    t = lax.axis_index("tile")
    krylov, parts, slab, ny, nz = basis.shape
    local = snapshots.shape[0]
    steps = local * groups
    rim = 3 * steps
    planes = slab + 2 * rim
    near = spans(slab, rim)
    offsets = sorted(near)
    position = krylov - groups + g

    def at(group, offset):
        return {"grp": group, "tile": lax.rem(t + (offset % tiles), tiles)}

    barrier = pltpu.get_barrier_semaphore()

    def greet(r, carry):
        pl.semaphore_signal(barrier, inc=1, device_id=at(g, 0) | {"tile": lax.rem(t + r, tiles)}, device_id_type=MESH)
        return carry

    lax.fori_loop(1, tiles, greet, 0)
    def greet_group(other):
        def greet_one(r, carry):
            pl.semaphore_signal(
                barrier,
                inc=1,
                device_id={"grp": lax.rem(g + other, groups), "tile": lax.rem(t + r, tiles)},
                device_id_type=MESH,
            )
            return carry

        lax.fori_loop(0, tiles, greet_one, 0)

    for other in range(1, groups):
        greet_group(other)

    chunk = 8 if krylov % 8 == 0 else 1
    loads = []
    own = pltpu.make_async_copy(basis.at[position], start.at[:, pl.ds(rim, slab)], load_sem.at[0])
    own.start()
    for n in range(krylov // chunk):
        part = pl.ds(n * chunk, chunk)
        copy = pltpu.make_async_copy(basis.at[part], held.at[part], load_sem.at[1 + n])
        copy.start()
        loads.append(copy)

    for copy in loads:
        copy.wait()
    size = krylov * ny
    wide = jnp.concatenate(
        [held[:, c, x].reshape(size, nz) for c in range(parts) for x in range(slab)], axis=1
    )
    cross[...] = lax.dot_general(
        wide, wide, (((1,), (1,)), ((), ())), preferred_element_type=f32
    )
    line = lax.broadcasted_iota(jnp.int32, (size, size), 0)
    column = lax.broadcasted_iota(jnp.int32, (size, size), 1)
    kept = jnp.where(lax.rem(line, ny) == lax.rem(column, ny), cross[...], 0.0)
    kept = jnp.sum(kept.reshape(krylov, ny, size), axis=1)
    pick = (
        lax.broadcasted_iota(jnp.int32, (size, krylov), 0) // ny
        == lax.broadcasted_iota(jnp.int32, (size, krylov), 1)
    ).astype(f32)
    gram = jnp.dot(kept, pick, precision=HIGHEST, preferred_element_type=f32)
    blocks, height = gram_blocks(krylov, nz)
    gram_send[...] = jnp.concatenate(
        [gram[n * height : (n + 1) * height] for n in range(blocks)], axis=1
    )

    pl.semaphore_wait(barrier, tiles * groups - 1)

    def target(d, first, last):
        return pl.ds(rim + d * slab + first, last - first)

    start_copies = []
    for n, d in enumerate(offsets):
        first, last = near[d]
        start_copies.append(
            pltpu.make_async_remote_copy(
                src_ref=basis.at[position, :, pl.ds(first, last - first)],
                dst_ref=start.at[:, target(d, first, last)],
                send_sem=start_send.at[n],
                recv_sem=start_recv.at[n],
                device_id=at(g, -d),
                device_id_type=MESH,
            )
        )

    def snap_copy(s, n, d, other):
        first, last = (0, slab) if d == 0 else spans(slab, rim - 3 * s - 1)[d]
        return pltpu.make_async_remote_copy(
            src_ref=snapshots.at[s % local, :, pl.ds(first, last - first)],
            dst_ref=snap.at[s, :, target(d, first, last)],
            send_sem=snap_send.at[s % local, other, n],
            recv_sem=snap_recv.at[s, n],
            device_id=at(lax.rem(g + other, groups), -d),
            device_id_type=MESH,
        )

    def local_snap(s):
        return pltpu.make_async_copy(
            snapshots.at[s % local], snap.at[s, :, pl.ds(rim, slab)], load_sem.at[1 + krylov // chunk + s % local]
        )

    def snap_offsets(s):
        inside = spans(slab, rim - 3 * s - 1)
        return [(n, d) for n, d in enumerate([0] + offsets) if d == 0 or d in inside]

    def send_snap(s):
        @pl.when(g == s // local)
        def _():
            local_snap(s).start()
            for n, d in snap_offsets(s):
                for other in range(1 if d else groups):
                    if d or other:
                        snap_copy(s, n, d, other).start()

    def relay_copy(s, n, d, other):
        first, last = spans(slab, rim - 3 * s - 1)[d]
        cells = snap.at[s, :, target(d, first, last)]
        return pltpu.make_async_remote_copy(
            src_ref=cells,
            dst_ref=cells,
            send_sem=snap_send.at[s % local, other, n],
            recv_sem=snap_recv.at[s, n],
            device_id=at(lax.rem(g + other, groups), 0),
            device_id_type=MESH,
        )

    def relay(s):
        @pl.when(g == s // local)
        def _():
            for n, d in snap_offsets(s):
                if d:
                    snap_copy(s, n, d, 0).wait_recv()
                    for other in range(1, groups):
                        relay_copy(s, n, d, other).start()
            local_snap(s).wait()

    def receive(s):
        if groups > 1:
            @pl.when(g != s // local)
            def _():
                snap_copy(s, 0, 0, 1).wait_recv()
                for n, d in snap_offsets(s):
                    if d:
                        relay_copy(s, n, d, 1).wait_recv()

    for s in range(local):
        send_snap(s)
    for copy in start_copies:
        copy.start()
    for s in range(local, steps):
        send_snap(s)

    def share(send, everyone, ssem, rsem):
        def copy(r):
            return pltpu.make_async_remote_copy(
                src_ref=send,
                dst_ref=everyone.at[t],
                send_sem=ssem.at[r],
                recv_sem=rsem.at[r],
                device_id={"grp": g, "tile": lax.rem(t + r, tiles)},
                device_id_type=MESH,
            )

        def begin():
            lax.fori_loop(1, tiles, lambda r, c: (copy(r).start(), c)[1], 0)
            everyone[t] = send[...]

        def arrive():
            def one_wait(r, c):
                pltpu.make_async_remote_copy(
                    src_ref=send,
                    dst_ref=everyone.at[lax.rem(t - r + tiles, tiles)],
                    send_sem=ssem.at[r],
                    recv_sem=rsem.at[r],
                    device_id={"grp": g, "tile": lax.rem(t + r, tiles)},
                    device_id_type=MESH,
                ).wait_recv()
                return c
            lax.fori_loop(1, tiles, one_wait, 0)

        def drain():
            lax.fori_loop(1, tiles, lambda r, c: (copy(r).wait_send(), c)[1], 0)

        return begin, arrive, drain

    gram_begin, gram_arrive, gram_drain = share(gram_send, gram_all, gram_ssem, gram_rsem)

    def coef_copy(other, r, sender_group, sender):
        return pltpu.make_async_remote_copy(
            src_ref=coef_send,
            dst_ref=coef_all.at[sender_group, sender],
            send_sem=coef_ssem.at[other, r],
            recv_sem=coef_rsem.at[other, r],
            device_id={"grp": lax.rem(g + other, groups), "tile": lax.rem(t + r, tiles)},
            device_id_type=MESH,
        )

    def coef_each(act):
        def group(other):
            lax.fori_loop(0 if other else 1, tiles, lambda r, c: (act(other, r), c)[1], 0)

        for other in range(groups):
            group(other)

    def coef_receive(other, r):
        coef_copy(other, r, lax.rem(g - other + groups, groups), lax.rem(t - r + tiles, tiles)).wait_recv()

    gram_begin()

    relay(0)
    own.wait()
    for copy in start_copies:
        copy.wait_recv()

    def widen(p, carry):
        for k in range(parts):
            state[k, p] = start[k, p].astype(f32)
        return carry

    lax.fori_loop(0, planes, widen, 0)
    lo, hi = 0, planes
    for s in range(steps):
        receive(s)
        stage(state, state, one, snap, s, coupling, lo + 1, hi - 1, 0.0, 1.0)
        if s == 0:
            for later in range(1, steps):
                relay(later)
        stage(one, state, two, snap, s, coupling, lo + 2, hi - 2, 0.75, 0.25)
        stage(two, state, state, snap, s, coupling, lo + 3, hi - 3, 1.0 / 3.0, 2.0 / 3.0)
        lo, hi = lo + 3, hi - 3

    count = f32(parts * slab * ny * nz * tiles)

    def project(k, carry):
        total = jnp.zeros((ny, nz), f32)
        for c in range(parts):
            for x in range(slab):
                total = total + held[k, c, x].astype(f32) * state[c, rim + x]
        rows_k[pl.ds(k, 1), :] = jnp.sum(total, axis=0, keepdims=True)
        return carry

    lax.fori_loop(0, krylov, project, 0, unroll=4)
    ones = jnp.ones((8, nz), f32)
    inner = lax.dot_general(
        ones, rows_k[...], (((1,), (1,)), ((), ())), precision=HIGHEST, preferred_element_type=f32
    )
    own_square = jnp.zeros((ny, nz), f32)
    for c in range(parts):
        for x in range(slab):
            own_square = own_square + state[c, rim + x] * state[c, rim + x]
    own_square = jnp.sum(jnp.sum(own_square, axis=0, keepdims=True), axis=1, keepdims=True)
    coef_send[...] = jnp.concatenate(
        [inner[0:1], jnp.broadcast_to(own_square, (1, coef_send.shape[1] - krylov))], axis=1
    )
    coef_each(lambda other, r: coef_copy(other, r, g, t).start())
    coef_all[g, t] = coef_send[...]
    gram_arrive()
    packed = jnp.sum(gram_all[...], axis=0) / count
    gram = jnp.concatenate(
        [packed[:, n * krylov : (n + 1) * krylov] for n in range(blocks)], axis=0
    )
    coef_each(coef_receive)
    sums = [jnp.sum(coef_all[n], axis=0) / count for n in range(groups)]
    sums = jnp.concatenate(sums + [jnp.zeros((-groups % 8, sums[0].shape[1]), f32)], axis=0)
    first_rows = sums[:, :krylov]
    work_square = sums[:, krylov : krylov + 1]
    times = functools.partial(jnp.dot, precision=HIGHEST, preferred_element_type=f32)
    every = first_rows + (first_rows - times(first_rows, gram))
    linear = 2.0 * every * first_rows
    bent = every * times(every, gram)
    bound = 2.0 * jnp.abs(every * first_rows) + jnp.abs(every) * times(jnp.abs(every), jnp.abs(gram))
    square = work_square + jnp.sum(bent - linear, axis=1, keepdims=True)
    bound = work_square + jnp.sum(bound, axis=1, keepdims=True)
    group_row = lax.broadcasted_iota(jnp.int32, square.shape, 0)
    margin = jnp.where(group_row < groups, square - cancel_limit * bound, jnp.inf)
    margin_out[...] = jnp.broadcast_to(jnp.min(margin, axis=0, keepdims=True), margin_out.shape)
    square = jnp.sum(jnp.where(group_row == g, square, 0.0), axis=0, keepdims=True)
    square_out[...] = jnp.broadcast_to(square, square_out.shape)
    both = jnp.sum(jnp.where(group_row == g, every, 0.0), axis=0, keepdims=True)
    coef_out[...] = both[0:1]
    for k in range(krylov):
        spread[k] = jnp.broadcast_to(both[:, k : k + 1], (8, nz))

    def subtract(x, carry):
        for c in range(parts):
            value = state[c, rim + x]
            removed = jnp.zeros((ny // 8, 8, nz), f32)
            for k in range(krylov):
                removed = removed + spread[k][None] * held[k, c, x].astype(f32).reshape(ny // 8, 8, nz)
            value = value - removed.reshape(ny, nz)
            left[0, c, x] = value
        return carry

    lax.fori_loop(0, slab, subtract, 0)
    for copy in start_copies:
        copy.wait_send()
    for s in range(steps):
        @pl.when(g == s // local)
        def _():
            for n, d in snap_offsets(s):
                for other in range(groups):
                    if d and other:
                        relay_copy(s, n, d, other).wait_send()
                    elif d or other:
                        snap_copy(s, n, d, other).wait_send()
    gram_drain()
    coef_each(lambda other, r: coef_copy(other, r, g, t).wait_send())


def square_kernel(tiles, left, square_out, send, everyone, ssem, rsem):
    g = lax.axis_index("grp")
    t = lax.axis_index("tile")
    _, parts, slab, ny, nz = left.shape
    barrier = pltpu.get_barrier_semaphore()

    def peer(r):
        return {"grp": g, "tile": lax.rem(t + r, tiles)}

    def greet(r, carry):
        pl.semaphore_signal(barrier, inc=1, device_id=peer(r), device_id_type=MESH)
        return carry

    lax.fori_loop(1, tiles, greet, 0)
    pl.semaphore_wait(barrier, tiles - 1)
    total = jnp.zeros((ny, nz), f32)
    for c in range(parts):
        for x in range(slab):
            total = total + left[0, c, x] * left[0, c, x]
    send[...] = jnp.sum(total, axis=0, keepdims=True)

    def copy(r, sender):
        return pltpu.make_async_remote_copy(
            src_ref=send,
            dst_ref=everyone.at[sender],
            send_sem=ssem.at[r],
            recv_sem=rsem.at[r],
            device_id=peer(r),
            device_id_type=MESH,
        )

    lax.fori_loop(1, tiles, lambda r, c: (copy(r, t).start(), c)[1], 0)
    everyone[t] = send[...]
    lax.fori_loop(
        1, tiles, lambda r, c: (copy(r, lax.rem(t - r + tiles, tiles)).wait_recv(), c)[1], 0
    )
    count = f32(parts * slab * ny * nz * tiles)
    square = jnp.sum(jnp.sum(everyone[...], axis=0), axis=1, keepdims=True) / count
    square_out[...] = jnp.broadcast_to(square, square_out.shape)
    lax.fori_loop(1, tiles, lambda r, c: (copy(r, t).wait_send(), c)[1], 0)


def finish(left, coefs, square, out, coef_out, norm_out):
    norm = jnp.sqrt(square[...])
    norm_out[...] = norm
    coef_out[...] = coefs[...]
    inverse = jnp.broadcast_to(1.0 / norm, left.shape[3:])
    for c in range(left.shape[1]):
        for x in range(left.shape[2]):
            out[0, c, x] = left[0, c, x] * inverse


def on_device(groups, tiles, basis, snapshots, coupling):
    krylov, parts, slab, ny, nz = basis.shape
    local, fields = snapshots.shape[:2]
    steps = local * groups
    rim = 3 * steps
    planes = slab + 2 * rim
    count = len(spans(slab, rim))
    blocks, height = gram_blocks(krylov, nz)
    dma = pltpu.SemaphoreType.DMA
    field = pltpu.VMEM((parts, planes, ny, nz), f32)
    whole = pl.BlockSpec(memory_space=pltpu.VMEM)
    results = pl.pallas_call(
        functools.partial(kernel, groups, tiles),
        name="propagate",
        out_shape=(
            jax.ShapeDtypeStruct((1, parts, slab, ny, nz), f32),
            jax.ShapeDtypeStruct((1, krylov), f32),
            jax.ShapeDtypeStruct((1, nz), f32),
            jax.ShapeDtypeStruct((1, nz), f32),
        ),
        in_specs=[
            pl.BlockSpec(memory_space=pltpu.SMEM),
            pl.BlockSpec(memory_space=pl.ANY),
            pl.BlockSpec(memory_space=pl.ANY),
        ],
        out_specs=(whole,) * 4,
        scratch_shapes=[
            pltpu.VMEM(basis.shape, bf16),
            pltpu.VMEM((parts, planes, ny, nz), bf16),
            pltpu.VMEM((steps, fields, planes, ny, nz), bf16),
            field,
            field,
            field,
            pltpu.VMEM((krylov * ny, krylov * ny), f32),
            pltpu.VMEM((krylov, nz), f32),
            pltpu.VMEM((krylov, 8, nz), f32),
            pltpu.VMEM((height, blocks * krylov), f32),
            pltpu.VMEM((tiles, height, blocks * krylov), f32),
            pltpu.VMEM((1, -(-(krylov + 1) // nz) * nz), f32),
            pltpu.VMEM((groups, tiles, 1, -(-(krylov + 1) // nz) * nz), f32),
            dma((1 + krylov + local,)),
            dma((count,)),
            dma((count,)),
            dma((local, groups, count + 1)),
            dma((steps, count + 1)),
            dma((tiles,)),
            dma((tiles,)),
            dma((groups, tiles)),
            dma((groups, tiles)),
        ],
        compiler_params=pltpu.CompilerParams(
            collective_id=0, has_side_effects=True, vmem_limit_bytes=67043328
        ),
    )(coupling, basis, snapshots)
    left, coefs, square, margin = results

    def scaled(left, coefs, square):
        return pl.pallas_call(
            finish,
            name="finish",
            out_shape=tuple(jax.ShapeDtypeStruct(a.shape, f32) for a in (left, coefs, square)),
            in_specs=[whole] * 3,
            out_specs=(whole, whole, whole),
        )(left, coefs, square)

    def summed(left, coefs, square):
        exact = pl.pallas_call(
            functools.partial(square_kernel, tiles),
            name="exact_square",
            out_shape=jax.ShapeDtypeStruct((1, nz), f32),
            in_specs=[whole],
            out_specs=whole,
            scratch_shapes=[
                pltpu.VMEM((1, nz), f32),
                pltpu.VMEM((tiles, 1, nz), f32),
                dma((tiles,)),
                dma((tiles,)),
            ],
            compiler_params=pltpu.CompilerParams(collective_id=1, has_side_effects=True),
        )(left)
        return scaled(left, coefs, exact)

    new_vector, coefs, norms = lax.cond(margin[0, 0] > 0.0, scaled, summed, left, coefs, square)
    return new_vector, coefs, norms[0, :1]


def solution(mesh):
    placed = (P(None, None, "tile", None, None), P("grp", None, "tile", None, None), P())
    return jax.shard_map(
        functools.partial(on_device, mesh.shape["grp"], mesh.shape["tile"]),
        mesh=mesh,
        in_specs=placed,
        out_specs=(P("grp", None, "tile", None, None), P("grp", None), P("grp")),
        check_vma=False,
    )
```

profile of v0, /device:TPU:0, one launch (start us, length us, event | category | flops | bytes accessed | tf_op | source)
XLA Modules:
  0.0 31.5 jit_solution(13881756211545433332)
XLA Ops:
  0.6 28.6 %propagate.1 = (f32[1,5,4,16,128]{4,3,2,1,0:T(8,128)}, f32[1,32]{1,0:T(1,128)}, f32[1,128]{1,0:T(1,128)}, f32[1,128]{1,0:T(1,128)}) custom-call(f32[5,5]{1,0:T(8,128)} %coupling.1, bf16[32,5,4,16,128]{4,3,2,1,0:T(8,128)(2,1)} %basis.1, bf16[1,4,4,16,128]{4,3,2,1,0:T(8,128)(2,1)} %snapshots.1), custom_call_target="tpu_custom_call" | custom-call | tf_op jit(solution)/shard_map/propagate/pallas_call | solution.py:454
  29.9 1.6 %conditional.1 = (f32[1,5,4,16,128]{4,3,2,1,0:T(8,128)}, f32[1,32]{1,0:T(1,128)}, f32[1]{0:T(128)}) conditional(s32[]{:T(128)} %bitcast.2, (f32[1,5,4,16,128]{4,3,2,1,0:T(8,128)}, f32[1,32]{1,0:T(1,128)}) %tuple.17, (f32[1,5,4,16,128]{4,3,2,1,0:T(8,128)}, f32[1,32]{1,0:T(1,128)}, f32[1,128]{1,0:T(1,128)}) %tuple.18), branch_computations={%region_0.0_spmd, %region_1.0_spmd} | conditional | bytes 24 | solution.py:525
  29.9 1.6 %finish.3 = (f32[1,5,4,16,128]{4,3,2,1,0:T(8,128)}, f32[1,32]{1,0:T(1,128)}, f32[1,128]{1,0:T(1,128)}) custom-call(f32[1,5,4,16,128]{4,3,2,1,0:T(8,128)} %get-tuple-element.22.left, f32[1,32]{1,0:T(1,128)} %get-tuple-element.23.coefs, f32[1,128]{1,0:T(1,128)} %get-tuple-element.24.square), custom_call_target="tpu_custom_call" | custom-call | tf_op jit(solution)/shard_map/cond/branch_1_fun/finish/pallas_call | solution.py:500
where the time goes:
time: 31.7 us; the launch traced here: 31.5 us
  Pallas kernels  30.2 us (95%)
  between operations  1.27 us (4%)
    pallas_call x1, Pallas kernels, on_device(): pl.pallas_call(functools.partial(kernel, groups, tiles), name='propagate'...  28.6 us
    pallas_call x1, Pallas kernels, scaled(): pl.pallas_call(finish, name='finish', out_shape=tuple((jax.ShapeDtypeStru...  1.62 us

commit v1 on v0

v1 whole, which is shorter than its diff:
```python
import functools

import jax
import jax.numpy as jnp
from jax import lax
from jax.experimental import pallas as pl
from jax.experimental.pallas import tpu as pltpu
from jax.sharding import PartitionSpec as P

viscosity = 0.5
time_step = 0.3
cancel_limit = 0.01
f32 = jnp.float32
bf16 = jnp.bfloat16
MESH = pl.DeviceIdType.MESH
HIGHEST = lax.Precision.HIGHEST


def spans(slab, rim):
    found = {}
    reach = -(-rim // slab)
    for d in range(1, reach + 1):
        width = min(slab, rim - (d - 1) * slab)
        found[-d] = (slab - width, slab)
        found[d] = (0, width)
    return found


def gram_blocks(krylov, lanes):
    blocks = max(lanes // krylov, 1)
    return (blocks, krylov // blocks) if krylov % (8 * blocks) == 0 else (1, krylov)


def stage(src, old, dst, snap, step, coupling, lo, hi, keep, gain):
    rows, lanes = src.shape[2], src.shape[3]
    row = lax.broadcasted_iota(jnp.int32, (rows, lanes), 0)
    first = row == 0
    last = row == rows - 1
    step_gain = time_step * gain
    mix = [[coupling[k, j] for j in range(5)] for k in range(5)]

    def body(i, carry):
        p = lo + i
        base = [snap[step, n, p].astype(f32) for n in range(4)]
        half = [(0.5 * step_gain) * base[n] for n in range(3)]
        edge = viscosity * step_gain
        x_up, x_low = edge - half[0], edge + half[0]
        y_up = jnp.where(last, 0.0, edge - half[1])
        y_low = jnp.where(first, 0.0, edge + half[1])
        z_up, z_low = edge - half[2], edge + half[2]
        pull = step_gain * base[3]
        center = [src[k, p] for k in range(5)]
        own = gain - 6.0 * viscosity * step_gain
        for k in range(5):
            q = center[k]
            coupled = mix[k][0] * center[0]
            for j in range(1, 5):
                coupled = coupled + mix[k][j] * center[j]
            total = own * q - pull * coupled
            total = total + (x_up * src[k, p + 1] + x_low * src[k, p - 1])
            total = total + (y_up * pltpu.roll(q, rows - 1, 0) + y_low * pltpu.roll(q, 1, 0))
            total = total + (z_up * pltpu.roll(q, lanes - 1, 1) + z_low * pltpu.roll(q, 1, 1))
            if keep:
                total = total + keep * old[k, p]
            dst[k, p] = total
        return carry

    lax.fori_loop(0, hi - lo, body, 0, unroll=4)


def kernel(
    groups, tiles, coupling_in, basis, snapshots,
    left_out, coef_out, square_out, margin_out,
    coupling, held, plain, start, snap, state, one, two, left, cross, rows_k, spread,
    gram_send, gram_all, coef_send, coef_all, margin_send, margin_all, coefs, square_row, margin_row,
    load_sem, start_send, start_recv, snap_send, snap_recv,
    share_send, share_recv, margin_ssem, margin_rsem, out_sem, ready,
):
    g = lax.axis_index("grp")
    t = lax.axis_index("tile")
    krylov, parts, slab, ny, nz = basis.shape
    local = snapshots.shape[0]
    steps = local * groups
    rim = 3 * steps
    planes = slab + 2 * rim
    near = spans(slab, rim)
    offsets = sorted(near)
    position = krylov - groups + g
    levels = [b for b in range(tiles.bit_length() - 1) if (1 << b) in offsets]
    stride = 1 << len(levels)
    length = tiles // stride
    link = t // stride

    def at(group, offset):
        return {"grp": group, "tile": lax.rem(t + (offset % tiles), tiles)}

    def flipped(level):
        bit = 1 << level
        return {"grp": g, "tile": t + bit - 2 * bit * lax.rem(t // bit, 2)}

    def partner(other):
        return {"grp": lax.rem(g + other, groups), "tile": t}

    barrier = pltpu.get_barrier_semaphore()
    greeted = [at(g, -d) for d in offsets] + [partner(other) for other in range(1, groups)]
    if length > 1:
        greeted += [at(g, stride), at(g, -stride)]
    for peer in greeted:
        pl.semaphore_signal(barrier, inc=1, device_id=peer, device_id_type=MESH)

    chunk = 8 if krylov % 8 == 0 else 1
    loads = []
    own = pltpu.make_async_copy(basis.at[position], start.at[:, pl.ds(rim, slab)], load_sem.at[0])
    own.start()
    mix = pltpu.make_async_copy(coupling_in, coupling, load_sem.at[1])
    mix.start()
    for n in range(krylov // chunk):
        part = pl.ds(n * chunk, chunk)
        copy = pltpu.make_async_copy(basis.at[part], held.at[part], load_sem.at[2 + n])
        copy.start()
        loads.append(copy)

    def target(d, first, last):
        return pl.ds(rim + d * slab + first, last - first)

    start_copies = []
    for n, d in enumerate(offsets):
        first, last = near[d]
        start_copies.append(
            pltpu.make_async_remote_copy(
                src_ref=basis.at[position, :, pl.ds(first, last - first)],
                dst_ref=start.at[:, target(d, first, last)],
                send_sem=start_send.at[n],
                recv_sem=start_recv.at[n],
                device_id=at(g, -d),
                device_id_type=MESH,
            )
        )

    def snap_copy(s, n, d, other):
        first, last = (0, slab) if d == 0 else spans(slab, rim - 3 * s - 1)[d]
        return pltpu.make_async_remote_copy(
            src_ref=snapshots.at[s % local, :, pl.ds(first, last - first)],
            dst_ref=snap.at[s, :, target(d, first, last)],
            send_sem=snap_send.at[s % local, other, n],
            recv_sem=snap_recv.at[s, n],
            device_id=at(lax.rem(g + other, groups), -d),
            device_id_type=MESH,
        )

    def local_snap(s):
        return pltpu.make_async_copy(
            snapshots.at[s % local], snap.at[s, :, pl.ds(rim, slab)], load_sem.at[2 + krylov // chunk + s % local]
        )

    def snap_offsets(s):
        inside = spans(slab, rim - 3 * s - 1)
        return [(n, d) for n, d in enumerate([0] + offsets) if d == 0 or d in inside]

    def send_snap(s):
        @pl.when(g == s // local)
        def _():
            for n, d in snap_offsets(s):
                for other in range(1 if d else groups):
                    if d or other:
                        snap_copy(s, n, d, other).start()

    def relay_copy(s, n, d, other):
        first, last = spans(slab, rim - 3 * s - 1)[d]
        cells = snap.at[s, :, target(d, first, last)]
        return pltpu.make_async_remote_copy(
            src_ref=cells,
            dst_ref=cells,
            send_sem=snap_send.at[s % local, other, n],
            recv_sem=snap_recv.at[s, n],
            device_id=at(lax.rem(g + other, groups), 0),
            device_id_type=MESH,
        )

    def relay(s):
        @pl.when(g == s // local)
        def _():
            for n, d in snap_offsets(s):
                if d:
                    snap_copy(s, n, d, 0).wait_recv()
                    for other in range(1, groups):
                        relay_copy(s, n, d, other).start()
            local_snap(s).wait()

    def receive(s):
        if groups > 1:
            @pl.when(g != s // local)
            def _():
                snap_copy(s, 0, 0, 1).wait_recv()
                for n, d in snap_offsets(s):
                    if d:
                        relay_copy(s, n, d, 1).wait_recv()

    for s in range(steps):
        @pl.when(g == s // local)
        def _():
            local_snap(s).start()

    pl.semaphore_wait(barrier, len(greeted))
    for s in range(local):
        send_snap(s)
    for copy in start_copies:
        copy.start()
    for s in range(local, steps):
        send_snap(s)

    def tell(n, peer):
        pl.semaphore_signal(ready.at[n], inc=1, device_id=peer, device_id_type=MESH)

    def flip_step(n):
        if n:
            pl.semaphore_wait(ready.at[n - 1], 1)
        if n < len(levels):
            tell(n, flipped(levels[n]))

    def pass_on(sem, way):
        head = link == (0 if way > 0 else length - 1)
        tail = link == (length - 1 if way > 0 else 0)

        @pl.when(jnp.logical_not(head))
        def _():
            pl.semaphore_wait(ready.at[sem], 1)

        @pl.when(jnp.logical_not(tail))
        def _():
            tell(sem, at(g, way * stride))

    def chain_step(n):
        if length > 1:
            upper = link >= length // 2
            for way in (1, -1):
                @pl.when(upper == (way < 0))
                def _():
                    mine = -way if n else way
                    pass_on(len(levels) + (mine < 0), mine)

    pending = [functools.partial(flip_step, n) for n in range(len(levels) + 1)]
    pending += [functools.partial(chain_step, n) for n in range(2)]
    pending.pop(0)()

    def advance():
        if pending:
            pending.pop(0)()

    for copy in loads:
        copy.wait()
    size = krylov * ny
    for c in range(parts):
        wide = jnp.concatenate([held[:, c, x].reshape(size, nz) for x in range(slab)], axis=1)
        piece = lax.dot_general(wide, wide, (((1,), (1,)), ((), ())), preferred_element_type=f32)
        cross[...] = cross[...] + piece if c else piece
        advance()
    line = lax.broadcasted_iota(jnp.int32, (size, size), 0)
    column = lax.broadcasted_iota(jnp.int32, (size, size), 1)
    kept = jnp.where(lax.rem(line, ny) == lax.rem(column, ny), cross[...], 0.0)
    kept = jnp.sum(kept.reshape(krylov, ny, size), axis=1)
    pick = (
        lax.broadcasted_iota(jnp.int32, (size, krylov), 0) // ny
        == lax.broadcasted_iota(jnp.int32, (size, krylov), 1)
    ).astype(f32)
    gram = jnp.dot(kept, pick, precision=HIGHEST, preferred_element_type=f32)
    blocks, height = gram_blocks(krylov, nz)
    gram_send[...] = jnp.concatenate(
        [gram[n * height : (n + 1) * height] for n in range(blocks)], axis=1
    )
    while pending:
        advance()

    def spread_out(n, send, everyone):
        way = 2 * (t // max(tiles // 2, 1)) - 1
        others = everyone.at[pl.ds(0, tiles - 1)]

        def begin():
            def one(i, carry):
                peer = lax.rem(2 * tiles - 1 - t + way * i, tiles)

                @pl.when(peer != t)
                def _():
                    pltpu.make_async_remote_copy(
                        src_ref=send,
                        dst_ref=everyone.at[t],
                        send_sem=share_send.at[n],
                        recv_sem=share_recv.at[n],
                        device_id={"grp": g, "tile": peer},
                        device_id_type=MESH,
                    ).start()

                return carry

            lax.fori_loop(0, tiles, one, 0)
            everyone[t] = send[...]

        def arrive():
            pltpu.make_async_copy(others, others, share_recv.at[n]).wait()

        def drain():
            pltpu.make_async_copy(others, others, share_send.at[n]).wait()

        return begin, arrive, drain

    gram_begin, gram_arrive, gram_drain = spread_out(0, gram_send, gram_all)
    coef_begin, coef_arrive, coef_drain = spread_out(1, coef_send, coef_all)
    gram_begin()

    def expand(k, carry):
        plain[k] = held[k].astype(f32)
        return carry

    lax.fori_loop(0, krylov, expand, 0)

    relay(0)
    own.wait()
    for copy in start_copies:
        copy.wait_recv()
    mix.wait()

    def widen(p, carry):
        for k in range(parts):
            state[k, p] = start[k, p].astype(f32)
        return carry

    lax.fori_loop(0, planes, widen, 0)
    lo, hi = 0, planes
    for s in range(steps):
        receive(s)
        stage(state, state, one, snap, s, coupling, lo + 1, hi - 1, 0.0, 1.0)
        if s == 0:
            for later in range(1, steps):
                relay(later)
        stage(one, state, two, snap, s, coupling, lo + 2, hi - 2, 0.75, 0.25)
        stage(two, state, state, snap, s, coupling, lo + 3, hi - 3, 1.0 / 3.0, 2.0 / 3.0)
        lo, hi = lo + 3, hi - 3

    count = f32(parts * slab * ny * nz * tiles)

    group = 4 if krylov % 4 == 0 else 1

    def project(i, carry):
        totals = [jnp.zeros((ny, nz), f32) for _ in range(group)]
        for c in range(parts):
            for x in range(slab):
                field = state[c, rim + x]
                for n in range(group):
                    totals[n] = totals[n] + plain[i * group + n, c, x] * field
        for n in range(group):
            rows_k[pl.ds(i * group + n, 1), :] = jnp.sum(totals[n], axis=0, keepdims=True)
        return carry

    lax.fori_loop(0, krylov // group, project, 0)
    ones = jnp.ones((8, nz), f32)
    inner = lax.dot_general(
        ones, rows_k[...], (((1,), (1,)), ((), ())), precision=HIGHEST, preferred_element_type=f32
    )
    own_square = jnp.zeros((ny, nz), f32)
    for c in range(parts):
        for x in range(slab):
            own_square = own_square + state[c, rim + x] * state[c, rim + x]
    own_square = jnp.sum(jnp.sum(own_square, axis=0, keepdims=True), axis=1, keepdims=True)
    coef_send[...] = jnp.concatenate(
        [inner[0:1], jnp.broadcast_to(own_square, (1, coef_send.shape[1] - krylov))], axis=1
    )
    coef_begin()
    for copy in start_copies:
        copy.wait_send()
    for s in range(steps):
        @pl.when(g == s // local)
        def _():
            for n, d in snap_offsets(s):
                for other in range(groups):
                    if d and other:
                        relay_copy(s, n, d, other).wait_send()
                    elif d or other:
                        snap_copy(s, n, d, other).wait_send()
    gram_drain()
    gram_arrive()
    packed = jnp.sum(gram_all[...], axis=0) / count
    gram = jnp.concatenate(
        [packed[:, n * krylov : (n + 1) * krylov] for n in range(blocks)], axis=0
    )
    same = lax.broadcasted_iota(jnp.int32, gram.shape, 0) == lax.broadcasted_iota(jnp.int32, gram.shape, 1)
    times = functools.partial(jnp.dot, precision=HIGHEST, preferred_element_type=f32)
    twice = jnp.where(same, 2.0, 0.0) - gram
    both = jnp.concatenate([twice, times(twice, gram)], axis=1)
    coef_arrive()
    sums = jnp.sum(coef_all[...], axis=0) / count
    first_row = jnp.broadcast_to(sums, (8, sums.shape[1]))
    work_square = first_row[:, krylov : krylov + 1]
    first_row = first_row[:, :krylov]
    mixed = times(first_row, both)
    every, turned = mixed[:, :krylov], mixed[:, krylov:]
    for k in range(krylov):
        spread[k] = jnp.broadcast_to(every[:, k : k + 1], (8, nz))
    linear = 2.0 * every * first_row
    bent = every * turned
    bound = 2.0 * jnp.abs(every * first_row) + jnp.abs(every) * times(jnp.abs(every), jnp.abs(gram))
    square = work_square + jnp.sum(bent - linear, axis=1, keepdims=True)
    bound = work_square + jnp.sum(bound, axis=1, keepdims=True)
    margin = square - cancel_limit * bound
    margin_send[...] = jnp.broadcast_to(margin[0:1], margin_send.shape)

    def margin_copy(other, sender):
        return pltpu.make_async_remote_copy(
            src_ref=margin_send,
            dst_ref=margin_all.at[sender],
            send_sem=margin_ssem.at[other],
            recv_sem=margin_rsem.at[other],
            device_id=partner(other),
            device_id_type=MESH,
        )

    for other in range(1, groups):
        margin_copy(other, g).start()
    margin_all[g] = margin_send[...]

    square_row[...] = jnp.broadcast_to(square[0:1], square_row.shape)
    coefs[...] = every[0:1]
    outs = [
        pltpu.make_async_copy(coefs, coef_out, out_sem.at[0]),
        pltpu.make_async_copy(square_row, square_out, out_sem.at[1]),
    ]
    for copy in outs:
        copy.start()
    for x in range(slab):
        removed = [jnp.zeros((ny // 8, 8, nz), f32) for _ in range(parts)]
        for k in range(krylov):
            factor = spread[k][None]
            for c in range(parts):
                removed[c] = removed[c] + factor * plain[k, c, x].reshape(ny // 8, 8, nz)
        for c in range(parts):
            left[c, x] = state[c, rim + x] - removed[c].reshape(ny, nz)
        copy = pltpu.make_async_copy(left.at[:, x], left_out.at[0, :, x], out_sem.at[3 + x])
        copy.start()
        outs.append(copy)
    for other in range(1, groups):
        margin_copy(other, lax.rem(g - other + groups, groups)).wait_recv()
    margin_row[...] = jnp.min(margin_all[...], axis=0)
    copy = pltpu.make_async_copy(margin_row, margin_out, out_sem.at[2])
    copy.start()
    outs.append(copy)
    coef_drain()
    for other in range(1, groups):
        margin_copy(other, g).wait_send()
    for copy in outs:
        copy.wait()


def square_kernel(tiles, left, square_out, send, everyone, ssem, rsem):
    g = lax.axis_index("grp")
    t = lax.axis_index("tile")
    _, parts, slab, ny, nz = left.shape
    barrier = pltpu.get_barrier_semaphore()

    def peer(r):
        return {"grp": g, "tile": lax.rem(t + r, tiles)}

    def greet(r, carry):
        pl.semaphore_signal(barrier, inc=1, device_id=peer(r), device_id_type=MESH)
        return carry

    lax.fori_loop(1, tiles, greet, 0)
    pl.semaphore_wait(barrier, tiles - 1)
    total = jnp.zeros((ny, nz), f32)
    for c in range(parts):
        for x in range(slab):
            total = total + left[0, c, x] * left[0, c, x]
    send[...] = jnp.sum(total, axis=0, keepdims=True)

    def copy(r, sender):
        return pltpu.make_async_remote_copy(
            src_ref=send,
            dst_ref=everyone.at[sender],
            send_sem=ssem.at[r],
            recv_sem=rsem.at[r],
            device_id=peer(r),
            device_id_type=MESH,
        )

    lax.fori_loop(1, tiles, lambda r, c: (copy(r, t).start(), c)[1], 0)
    everyone[t] = send[...]
    lax.fori_loop(
        1, tiles, lambda r, c: (copy(r, lax.rem(t - r + tiles, tiles)).wait_recv(), c)[1], 0
    )
    count = f32(parts * slab * ny * nz * tiles)
    square = jnp.sum(jnp.sum(everyone[...], axis=0), axis=1, keepdims=True) / count
    square_out[...] = jnp.broadcast_to(square, square_out.shape)
    lax.fori_loop(1, tiles, lambda r, c: (copy(r, t).wait_send(), c)[1], 0)


def finish(left, coefs, square, out, coef_out, norm_out, held, row, norm_row, line, sem):
    loads = [
        pltpu.make_async_copy(square, row, sem.at[0]),
        pltpu.make_async_copy(left, held, sem.at[1]),
        pltpu.make_async_copy(coefs, line, sem.at[2]),
    ]
    for copy in loads:
        copy.start()
    loads[0].wait()
    norm = jnp.sqrt(row[...])
    norm_row[...] = norm
    loads[2].wait()
    stores = [
        pltpu.make_async_copy(norm_row, norm_out, sem.at[0]),
        pltpu.make_async_copy(line, coef_out, sem.at[2]),
    ]
    for copy in stores:
        copy.start()
    inverse = jnp.broadcast_to(1.0 / norm, left.shape[3:])
    loads[1].wait()
    for c in range(left.shape[1]):
        for x in range(left.shape[2]):
            held[0, c, x] = held[0, c, x] * inverse
    last = pltpu.make_async_copy(held, out, sem.at[1])
    last.start()
    for copy in stores:
        copy.wait()
    last.wait()


def on_device(groups, tiles, basis, snapshots, coupling):
    krylov, parts, slab, ny, nz = basis.shape
    local, fields = snapshots.shape[:2]
    steps = local * groups
    rim = 3 * steps
    planes = slab + 2 * rim
    count = len(spans(slab, rim))
    blocks, height = gram_blocks(krylov, nz)
    width = -(-(krylov + 1) // nz) * nz
    dma = pltpu.SemaphoreType.DMA
    field = pltpu.VMEM((parts, planes, ny, nz), f32)
    whole = pl.BlockSpec(memory_space=pltpu.VMEM)
    anywhere = pl.BlockSpec(memory_space=pl.ANY)
    results = pl.pallas_call(
        functools.partial(kernel, groups, tiles),
        name="propagate",
        out_shape=(
            jax.ShapeDtypeStruct((1, parts, slab, ny, nz), f32),
            jax.ShapeDtypeStruct((1, krylov), f32),
            jax.ShapeDtypeStruct((1, nz), f32),
            jax.ShapeDtypeStruct((1, nz), f32),
        ),
        in_specs=[anywhere] * 3,
        out_specs=(anywhere,) * 4,
        scratch_shapes=[
            pltpu.SMEM(coupling.shape, f32),
            pltpu.VMEM(basis.shape, bf16),
            pltpu.VMEM(basis.shape, f32),
            pltpu.VMEM((parts, planes, ny, nz), bf16),
            pltpu.VMEM((steps, fields, planes, ny, nz), bf16),
            field,
            field,
            field,
            pltpu.VMEM((parts, slab, ny, nz), f32),
            pltpu.VMEM((krylov * ny, krylov * ny), f32),
            pltpu.VMEM((krylov, nz), f32),
            pltpu.VMEM((krylov, 8, nz), f32),
            pltpu.VMEM((height, blocks * krylov), f32),
            pltpu.VMEM((tiles, height, blocks * krylov), f32),
            pltpu.VMEM((1, width), f32),
            pltpu.VMEM((tiles, 1, width), f32),
            pltpu.VMEM((1, nz), f32),
            pltpu.VMEM((groups, 1, nz), f32),
            pltpu.VMEM((1, krylov), f32),
            pltpu.VMEM((1, nz), f32),
            pltpu.VMEM((1, nz), f32),
            dma((2 + (krylov // 8 if krylov % 8 == 0 else krylov) + local,)),
            dma((count,)),
            dma((count,)),
            dma((local, groups, count + 1)),
            dma((steps, count + 1)),
            dma((2,)),
            dma((2,)),
            dma((groups,)),
            dma((groups,)),
            dma((slab + 3,)),
            pltpu.SemaphoreType.REGULAR((tiles.bit_length() + 2,)),
        ],
        compiler_params=pltpu.CompilerParams(
            collective_id=0, has_side_effects=True, vmem_limit_bytes=67043328
        ),
    )(coupling, basis, snapshots)
    left, coefs, square, margin = results

    def scaled(left, coefs, square):
        return pl.pallas_call(
            finish,
            name="finish",
            out_shape=tuple(jax.ShapeDtypeStruct(a.shape, f32) for a in (left, coefs, square)),
            in_specs=[anywhere] * 3,
            out_specs=(anywhere,) * 3,
            scratch_shapes=[
                pltpu.VMEM(left.shape, f32),
                pltpu.VMEM(square.shape, f32),
                pltpu.VMEM(square.shape, f32),
                pltpu.VMEM(coefs.shape, f32),
                dma((3,)),
            ],
        )(left, coefs, square)

    def summed(left, coefs, square):
        exact = pl.pallas_call(
            functools.partial(square_kernel, tiles),
            name="exact_square",
            out_shape=jax.ShapeDtypeStruct((1, nz), f32),
            in_specs=[whole],
            out_specs=whole,
            scratch_shapes=[
                pltpu.VMEM((1, nz), f32),
                pltpu.VMEM((tiles, 1, nz), f32),
                dma((tiles,)),
                dma((tiles,)),
            ],
            compiler_params=pltpu.CompilerParams(collective_id=1, has_side_effects=True),
        )(left)
        return scaled(left, coefs, exact)

    new_vector, coefs, norms = lax.cond(margin[0, 0] > 0.0, scaled, summed, left, coefs, square)
    return new_vector, coefs, norms[0, :1]


def solution(mesh):
    placed = (P(None, None, "tile", None, None), P("grp", None, "tile", None, None), P())
    return jax.shard_map(
        functools.partial(on_device, mesh.shape["grp"], mesh.shape["tile"]),
        mesh=mesh,
        in_specs=placed,
        out_specs=(P("grp", None, "tile", None, None), P("grp", None), P("grp")),
        check_vma=False,
    )
```

time: 31.7 us -> 28.2 us (0.89)
  Pallas kernels: 30.2 us -> 26.5 us
    pallas_call x1, Pallas kernels: 28.6 us -> 24.9 us  [on_device(): pl.pallas_call(functools.partial(kernel, groups, tiles), name='propagate'...]
where the time goes in v1:
time: 28.2 us; the launch traced here: 27.8 us
  Pallas kernels  26.5 us (94%)
  between operations  1.27 us (5%)
    pallas_call x1, Pallas kernels, on_device(): pl.pallas_call(functools.partial(kernel, groups, tiles), name='propagate'...  24.9 us
    pallas_call x1, Pallas kernels, scaled(): pl.pallas_call(finish, name='finish', out_shape=tuple((jax.ShapeDtypeStru...  1.62 us

profile of v1, /device:TPU:0, one launch (start us, length us, event | category | flops | bytes accessed | tf_op | source)
XLA Modules:
  0.0 27.8 jit_solution(10853734124416534990)
XLA Ops:
  0.6 24.9 %propagate.1 = (f32[1,5,4,16,128]{4,3,2,1,0:T(8,128)}, f32[1,32]{1,0:T(1,128)}, f32[1,128]{1,0:T(1,128)}, f32[1,128]{1,0:T(1,128)}) custom-call(f32[5,5]{1,0:T(8,128)} %coupling_in.1, bf16[32,5,4,16,128]{4,3,2,1,0:T(8,128)(2,1)} %basis.1, bf16[1,4,4,16,128]{4,3,2,1,0:T(8,128)(2,1)} %snapshots.1), custom_call_target="tpu_custom_call" | custom-call | tf_op jit(solution)/shard_map/propagate/pallas_call | solution.py:537
  26.2 1.6 %conditional.1 = (f32[1,5,4,16,128]{4,3,2,1,0:T(8,128)}, f32[1,32]{1,0:T(1,128)}, f32[1]{0:T(128)}) conditional(s32[]{:T(128)} %bitcast.2, (f32[1,5,4,16,128]{4,3,2,1,0:T(8,128)}, f32[1,32]{1,0:T(1,128)}) %tuple.17, (f32[1,5,4,16,128]{4,3,2,1,0:T(8,128)}, f32[1,32]{1,0:T(1,128)}, f32[1,128]{1,0:T(1,128)}) %tuple.18), branch_computations={%region_0.0_spmd, %region_1.0_spmd} | conditional | bytes 24 | solution.py:621
  26.2 1.6 %finish.3 = (f32[1,5,4,16,128]{4,3,2,1,0:T(8,128)}, f32[1,32]{1,0:T(1,128)}, f32[1,128]{1,0:T(1,128)}) custom-call(f32[1,5,4,16,128]{4,3,2,1,0:T(8,128)} %get-tuple-element.22.left, f32[1,32]{1,0:T(1,128)} %get-tuple-element.23.coefs, f32[1,128]{1,0:T(1,128)} %get-tuple-element.24.square), custom_call_target="tpu_custom_call" | custom-call | tf_op jit(solution)/shard_map/cond/branch_1_fun/finish/pallas_call | solution.py:589

commit v2 on v1

--- a/solution.py
+++ b/solution.py
@@ -31,22 +31,21 @@
     return (blocks, krylov // blocks) if krylov % (8 * blocks) == 0 else (1, krylov)
 
 
-def stage(src, old, dst, snap, step, coupling, lo, hi, keep, gain):
+def stage(src, old, dst, snap, step, coupling, first_planes, planes, keep, gain):
     rows, lanes = src.shape[2], src.shape[3]
     row = lax.broadcasted_iota(jnp.int32, (rows, lanes), 0)
-    first = row == 0
+    top = row == 0
     last = row == rows - 1
     step_gain = time_step * gain
     mix = [[coupling[k, j] for j in range(5)] for k in range(5)]
 
-    def body(i, carry):
-        p = lo + i
+    def one_plane(p):
         base = [snap[step, n, p].astype(f32) for n in range(4)]
         half = [(0.5 * step_gain) * base[n] for n in range(3)]
         edge = viscosity * step_gain
         x_up, x_low = edge - half[0], edge + half[0]
         y_up = jnp.where(last, 0.0, edge - half[1])
-        y_low = jnp.where(first, 0.0, edge + half[1])
+        y_low = jnp.where(top, 0.0, edge + half[1])
         z_up, z_low = edge - half[2], edge + half[2]
         pull = step_gain * base[3]
         center = [src[k, p] for k in range(5)]
@@ -63,9 +62,14 @@
             if keep:
                 total = total + keep * old[k, p]
             dst[k, p] = total
+
+    def body(i, carry):
+        for lo in first_planes:
+            one_plane(lo + i)
         return carry
 
-    lax.fori_loop(0, hi - lo, body, 0, unroll=4)
+    unroll = max(n for n in range(1, 6) if planes % n == 0)
+    lax.fori_loop(0, planes, body, 0, unroll=unroll)
 
 
 def kernel(
@@ -73,7 +77,7 @@
     left_out, coef_out, square_out, margin_out,
     coupling, held, plain, start, snap, state, one, two, left, cross, rows_k, spread,
     gram_send, gram_all, coef_send, coef_all, margin_send, margin_all, coefs, square_row, margin_row,
-    load_sem, start_send, start_recv, snap_send, snap_recv,
+    load_sem, start_send, start_recv, snap_send, relay_send, snap_recv,
     share_send, share_recv, margin_ssem, margin_rsem, out_sem, ready,
 ):
     g = lax.axis_index("grp")
@@ -102,23 +106,38 @@
         return {"grp": lax.rem(g + other, groups), "tile": t}
 
     barrier = pltpu.get_barrier_semaphore()
-    greeted = [at(g, -d) for d in offsets] + [partner(other) for other in range(1, groups)]
-    if length > 1:
-        greeted += [at(g, stride), at(g, -stride)]
-    for peer in greeted:
+    def crosses(d):
+        return t + d >= tiles if d > 0 else t + d < 0
+
+    def greet(peer):
         pl.semaphore_signal(barrier, inc=1, device_id=peer, device_id_type=MESH)
 
+    greeters = groups - 1
+    for d in sorted(offsets, key=abs, reverse=True):
+        if d > 0:
+            greet(at(g, -d))
+            greeters = greeters + 1
+        else:
+            pl.when(jnp.logical_not(crosses(-d)))(functools.partial(greet, at(g, -d)))
+            greeters = greeters + jnp.where(crosses(d), 0, 1)
+    for other in range(1, groups):
+        greet(partner(other))
+    for way in (1, -1):
+        last = link == (length - 1 if way > 0 else 0)
+        greeters = greeters + jnp.where(last, 0, 1)
+
+        @pl.when(jnp.logical_not(last))
+        def _():
+            greet(at(g, way * stride))
+
     chunk = 8 if krylov % 8 == 0 else 1
-    loads = []
     own = pltpu.make_async_copy(basis.at[position], start.at[:, pl.ds(rim, slab)], load_sem.at[0])
     own.start()
     mix = pltpu.make_async_copy(coupling_in, coupling, load_sem.at[1])
     mix.start()
     for n in range(krylov // chunk):
         part = pl.ds(n * chunk, chunk)
-        copy = pltpu.make_async_copy(basis.at[part], held.at[part], load_sem.at[2 + n])
-        copy.start()
-        loads.append(copy)
+        pltpu.make_async_copy(basis.at[part], held.at[part], load_sem.at[2]).start()
 
     def target(d, first, last):
         return pl.ds(rim + d * slab + first, last - first)
@@ -130,7 +149,7 @@
             pltpu.make_async_remote_copy(
                 src_ref=basis.at[position, :, pl.ds(first, last - first)],
                 dst_ref=start.at[:, target(d, first, last)],
-                send_sem=start_send.at[n],
+                send_sem=start_send.at[0],
                 recv_sem=start_recv.at[n],
                 device_id=at(g, -d),
                 device_id_type=MESH,
@@ -142,7 +161,7 @@
         return pltpu.make_async_remote_copy(
             src_ref=snapshots.at[s % local, :, pl.ds(first, last - first)],
             dst_ref=snap.at[s, :, target(d, first, last)],
-            send_sem=snap_send.at[s % local, other, n],
+            send_sem=snap_send.at[s % local],
             recv_sem=snap_recv.at[s, n],
             device_id=at(lax.rem(g + other, groups), -d),
             device_id_type=MESH,
@@ -150,20 +169,23 @@
 
     def local_snap(s):
         return pltpu.make_async_copy(
-            snapshots.at[s % local], snap.at[s, :, pl.ds(rim, slab)], load_sem.at[2 + krylov // chunk + s % local]
+            snapshots.at[s % local], snap.at[s, :, pl.ds(rim, slab)], load_sem.at[3 + s % local]
         )
 
     def snap_offsets(s):
         inside = spans(slab, rim - 3 * s - 1)
         return [(n, d) for n, d in enumerate([0] + offsets) if d == 0 or d in inside]
 
-    def send_snap(s):
+    def snap_each(s, ds, act):
+        inside = {d: n for n, d in snap_offsets(s)}
+
         @pl.when(g == s // local)
         def _():
-            for n, d in snap_offsets(s):
-                for other in range(1 if d else groups):
-                    if d or other:
-                        snap_copy(s, n, d, other).start()
+            for d in ds:
+                if d in inside:
+                    for other in range(1 if d else groups):
+                        if d or other:
+                            act(snap_copy(s, inside[d], d, other))
 
     def relay_copy(s, n, d, other):
         first, last = spans(slab, rim - 3 * s - 1)[d]
@@ -171,46 +193,78 @@
         return pltpu.make_async_remote_copy(
             src_ref=cells,
             dst_ref=cells,
-            send_sem=snap_send.at[s % local, other, n],
+            send_sem=relay_send.at[s % local],
             recv_sem=snap_recv.at[s, n],
             device_id=at(lax.rem(g + other, groups), 0),
             device_id_type=MESH,
         )
 
-    def relay(s):
+    def relay(s, ds):
         @pl.when(g == s // local)
         def _():
             for n, d in snap_offsets(s):
-                if d:
+                if d and d in ds:
                     snap_copy(s, n, d, 0).wait_recv()
                     for other in range(1, groups):
                         relay_copy(s, n, d, other).start()
-            local_snap(s).wait()
-
-    def receive(s):
+            if 0 in ds:
+                local_snap(s).wait()
+
+    def receive(s, ds):
         if groups > 1:
             @pl.when(g != s // local)
             def _():
-                snap_copy(s, 0, 0, 1).wait_recv()
                 for n, d in snap_offsets(s):
-                    if d:
-                        relay_copy(s, n, d, 1).wait_recv()
+                    if d in ds:
+                        (relay_copy if d else snap_copy)(s, n, d, 1).wait_recv()
 
     for s in range(steps):
         @pl.when(g == s // local)
         def _():
             local_snap(s).start()
 
-    pl.semaphore_wait(barrier, len(greeted))
-    for s in range(local):
-        send_snap(s)
-    for copy in start_copies:
-        copy.start()
-    for s in range(local, steps):
-        send_snap(s)
+    pl.semaphore_wait(barrier, greeters)
+    def send(s, ds):
+        snap_each(s, ds, lambda copy: copy.start())
+        if s == 0:
+            for d in ds:
+                if d:
+                    start_copies[offsets.index(d)].start()
 
     def tell(n, peer):
         pl.semaphore_signal(ready.at[n], inc=1, device_id=peer, device_id_type=MESH)
+
+    edge = len(levels) + 3
+
+    for d in offsets:
+        if d < 0:
+            pl.when(crosses(-d))(functools.partial(tell, edge - d - 1, at(g, -d)))
+    upper = t >= tiles // 2
+    ahead = [d for d in offsets if d < 0]
+    back = [-d for d in ahead]
+
+    def send_near(s):
+        if s == 0:
+            snap_each(0, [0], lambda copy: copy.start())
+        else:
+            snap_each(s, [0], lambda copy: copy.start())
+        for d in sorted(offsets, key=abs):
+            if d < 0:
+                send(s, [d])
+            else:
+                pl.when(jnp.logical_not(crosses(-d)))(functools.partial(send, s, [d]))
+
+    def send_late():
+        for d in sorted(back):
+            @pl.when(crosses(-d))
+            def _():
+                pl.semaphore_wait(ready.at[edge + d - 1], 1)
+                send(0, [d])
+                for s in range(1, steps):
+                    send(s, [d])
+
+    for s in range(steps):
+        send_near(s)
 
     def flip_step(n):
         if n:
@@ -239,21 +293,34 @@
                     mine = -way if n else way
                     pass_on(len(levels) + (mine < 0), mine)
 
+    def tell_group():
+        for other in range(1, groups):
+            tell(len(levels) + 2, partner(other))
+
     pending = [functools.partial(flip_step, n) for n in range(len(levels) + 1)]
-    pending += [functools.partial(chain_step, n) for n in range(2)]
-    pending.pop(0)()
+    pending += [functools.partial(chain_step, n) for n in range(2)] + [tell_group]
 
     def advance():
         if pending:
-            pending.pop(0)()
-
-    for copy in loads:
-        copy.wait()
+            pl.when(g == groups - 1)(pending.pop(0))
+
+    def all_ready():
+        while pending:
+            advance()
+        if groups > 1:
+            @pl.when(g != groups - 1)
+            def _():
+                pl.semaphore_wait(ready.at[len(levels) + 2], 1)
+
+    advance()
+    pltpu.make_async_copy(basis, held, load_sem.at[2]).wait()
     size = krylov * ny
     for c in range(parts):
         wide = jnp.concatenate([held[:, c, x].reshape(size, nz) for x in range(slab)], axis=1)
         piece = lax.dot_general(wide, wide, (((1,), (1,)), ((), ())), preferred_element_type=f32)
         cross[...] = cross[...] + piece if c else piece
+        if c == min(3, parts - 1):
+            send_late()
         advance()
     line = lax.broadcasted_iota(jnp.int32, (size, size), 0)
     column = lax.broadcasted_iota(jnp.int32, (size, size), 1)
@@ -268,9 +335,6 @@
     gram_send[...] = jnp.concatenate(
         [gram[n * height : (n + 1) * height] for n in range(blocks)], axis=1
     )
-    while pending:
-        advance()
-
     def spread_out(n, send, everyone):
         way = 2 * (t // max(tiles // 2, 1)) - 1
         others = everyone.at[pl.ds(0, tiles - 1)]
@@ -305,7 +369,6 @@
 
     gram_begin, gram_arrive, gram_drain = spread_out(0, gram_send, gram_all)
     coef_begin, coef_arrive, coef_drain = spread_out(1, coef_send, coef_all)
-    gram_begin()
 
     def expand(k, carry):
         plain[k] = held[k].astype(f32)
@@ -313,28 +376,63 @@
 
     lax.fori_loop(0, krylov, expand, 0)
 
-    relay(0)
-    own.wait()
-    for copy in start_copies:
-        copy.wait_recv()
-    mix.wait()
-
-    def widen(p, carry):
-        for k in range(parts):
-            state[k, p] = start[k, p].astype(f32)
-        return carry
-
-    lax.fori_loop(0, planes, widen, 0)
-    lo, hi = 0, planes
-    for s in range(steps):
-        receive(s)
-        stage(state, state, one, snap, s, coupling, lo + 1, hi - 1, 0.0, 1.0)
-        if s == 0:
-            for later in range(1, steps):
-                relay(later)
-        stage(one, state, two, snap, s, coupling, lo + 2, hi - 2, 0.75, 0.25)
-        stage(two, state, state, snap, s, coupling, lo + 3, hi - 3, 1.0 / 3.0, 2.0 / 3.0)
-        lo, hi = lo + 3, hi - 3
+    def widen(d):
+        def one(p, carry):
+            for k in range(parts):
+                state[k, p] = start[k, p].astype(f32)
+            return carry
+
+        lo, width = (rim, slab) if d == 0 else (rim + d * slab + near[d][0], near[d][1] - near[d][0])
+        lax.fori_loop(lo, lo + width, one, 0)
+
+    def arrive(ds):
+        for d in ds:
+            if d:
+                start_copies[offsets.index(d)].wait_recv()
+            else:
+                own.wait()
+                mix.wait()
+            widen(d)
+
+    weights = ((0.0, 1.0), (0.75, 0.25), (1.0 / 3.0, 2.0 / 3.0))
+    ways = ((state, one), (one, two), (two, state))
+
+    def march(s, known, new):
+        for n, (src, dst) in enumerate(ways):
+            k = 3 * s + n + 1
+            lo, hi = max(k, known - k), new - k
+            if hi > lo:
+                first = jnp.where(upper, lo, planes - hi)
+                stage(src, state, dst, snap, s, coupling, [first], hi - lo, *weights[n])
+
+    def sided(act, *ds):
+        for way, on in ((1, upper), (-1, jnp.logical_not(upper))):
+            @pl.when(on)
+            def _():
+                act([way * d for d in ds])
+
+    near_ds, far_ds = sorted(ahead, key=abs), sorted(back)
+    sided(lambda ds: (relay(0, [0] + ds), arrive(ds)), *near_ds)
+    arrive([0])
+    for s in range(1, steps):
+        sided(lambda ds: relay(s, [0] + ds), *near_ds)
+    sided(lambda ds: receive(0, [0] + ds), *near_ds)
+    known = 0
+    for piece in range(len(far_ds) + 1):
+        if piece:
+            sided(lambda ds: (relay(0, ds), arrive(ds)), far_ds[piece - 1])
+            for s in range(1, steps):
+                sided(lambda ds: relay(s, ds), far_ds[piece - 1])
+            sided(lambda ds: receive(0, ds), far_ds[piece - 1])
+        new = rim + slab + sum(near[d][1] - near[d][0] for d in far_ds[:piece])
+        for s in range(steps):
+            if s:
+                sided(lambda ds: receive(s, ds), *(([0] + near_ds) if piece == 0 else far_ds[piece - 1 : piece]))
+            march(s, known, new)
+        known = new
+        if piece == 0:
+            all_ready()
+            gram_begin()
 
     count = f32(parts * slab * ny * nz * tiles)
 
@@ -365,17 +463,20 @@
         [inner[0:1], jnp.broadcast_to(own_square, (1, coef_send.shape[1] - krylov))], axis=1
     )
     coef_begin()
-    for copy in start_copies:
-        copy.wait_send()
+    def all_sent(cells, sem):
+        pltpu.make_async_copy(cells, cells, sem).wait()
+
+    all_sent(start.at[:, pl.ds(0, 2 * rim)], start_send.at[0])
     for s in range(steps):
+        around = 2 * (rim - 3 * s - 1)
+
         @pl.when(g == s // local)
         def _():
-            for n, d in snap_offsets(s):
-                for other in range(groups):
-                    if d and other:
-                        relay_copy(s, n, d, other).wait_send()
-                    elif d or other:
-                        snap_copy(s, n, d, other).wait_send()
+            all_sent(snap.at[s, :, pl.ds(0, around)], snap_send.at[s % local])
+            for other in range(1, groups):
+                all_sent(snap.at[s, :, pl.ds(0, slab)], snap_send.at[s % local])
+                all_sent(snap.at[s, :, pl.ds(0, around)], relay_send.at[s % local])
+
     gram_drain()
     gram_arrive()
     packed = jnp.sum(gram_all[...], axis=0) / count
@@ -433,9 +534,8 @@
                 removed[c] = removed[c] + factor * plain[k, c, x].reshape(ny // 8, 8, nz)
         for c in range(parts):
             left[c, x] = state[c, rim + x] - removed[c].reshape(ny, nz)
-        copy = pltpu.make_async_copy(left.at[:, x], left_out.at[0, :, x], out_sem.at[3 + x])
+        copy = pltpu.make_async_copy(left.at[:, x], left_out.at[0, :, x], out_sem.at[3])
         copy.start()
-        outs.append(copy)
     for other in range(1, groups):
         margin_copy(other, lax.rem(g - other + groups, groups)).wait_recv()
     margin_row[...] = jnp.min(margin_all[...], axis=0)
@@ -447,6 +547,7 @@
         margin_copy(other, g).wait_send()
     for copy in outs:
         copy.wait()
+    pltpu.make_async_copy(left, left_out.at[0], out_sem.at[3]).wait()
 
 
 def square_kernel(tiles, left, square_out, send, everyone, ssem, rsem):
@@ -567,17 +668,18 @@
             pltpu.VMEM((1, krylov), f32),
             pltpu.VMEM((1, nz), f32),
             pltpu.VMEM((1, nz), f32),
-            dma((2 + (krylov // 8 if krylov % 8 == 0 else krylov) + local,)),
+            dma((3 + local,)),
+            dma((1,)),
             dma((count,)),
-            dma((count,)),
-            dma((local, groups, count + 1)),
+            dma((local,)),
+            dma((local,)),
             dma((steps, count + 1)),
             dma((2,)),
             dma((2,)),
             dma((groups,)),
             dma((groups,)),
-            dma((slab + 3,)),
-            pltpu.SemaphoreType.REGULAR((tiles.bit_length() + 2,)),
+            dma((4,)),
+            pltpu.SemaphoreType.REGULAR((tiles.bit_length() + 2 + -(-rim // slab),)),
         ],
         compiler_params=pltpu.CompilerParams(
             collective_id=0, has_side_effects=True, vmem_limit_bytes=67043328

time: 28.2 us -> 26.8 us (0.950)
  Pallas kernels: 26.5 us -> 25.3 us
    pallas_call x1, Pallas kernels: 24.9 us -> 23.7 us  [on_device(): pl.pallas_call(functools.partial(kernel, groups, tiles), name='propagate'...]
where the time goes in v2:
time: 26.8 us; the launch traced here: 26.6 us
  Pallas kernels  25.3 us (94%)
  between operations  1.27 us (5%)
    pallas_call x1, Pallas kernels, on_device(): pl.pallas_call(functools.partial(kernel, groups, tiles), name='propagate'...  23.7 us
    pallas_call x1, Pallas kernels, scaled(): pl.pallas_call(finish, name='finish', out_shape=tuple((jax.ShapeDtypeStru...  1.62 us

profile of v2, /device:TPU:0, one launch (start us, length us, event | category | flops | bytes accessed | tf_op | source)
XLA Modules:
  0.0 26.6 jit_solution(3327945518170288929)
XLA Ops:
  0.6 23.7 %propagate.1 = (f32[1,5,4,16,128]{4,3,2,1,0:T(8,128)}, f32[1,32]{1,0:T(1,128)}, f32[1,128]{1,0:T(1,128)}, f32[1,128]{1,0:T(1,128)}) custom-call(f32[5,5]{1,0:T(8,128)} %coupling_in.1, bf16[32,5,4,16,128]{4,3,2,1,0:T(8,128)(2,1)} %basis.1, bf16[1,4,4,16,128]{4,3,2,1,0:T(8,128)(2,1)} %snapshots.1), custom_call_target="tpu_custom_call" | custom-call | tf_op jit(solution)/shard_map/propagate/pallas_call | solution.py:638
  25.0 1.6 %conditional.1 = (f32[1,5,4,16,128]{4,3,2,1,0:T(8,128)}, f32[1,32]{1,0:T(1,128)}, f32[1]{0:T(128)}) conditional(s32[]{:T(128)} %bitcast.2, (f32[1,5,4,16,128]{4,3,2,1,0:T(8,128)}, f32[1,32]{1,0:T(1,128)}) %tuple.17, (f32[1,5,4,16,128]{4,3,2,1,0:T(8,128)}, f32[1,32]{1,0:T(1,128)}, f32[1,128]{1,0:T(1,128)}) %tuple.18), branch_computations={%region_0.0_spmd, %region_1.0_spmd} | conditional | bytes 24 | solution.py:723
  25.0 1.6 %finish.3 = (f32[1,5,4,16,128]{4,3,2,1,0:T(8,128)}, f32[1,32]{1,0:T(1,128)}, f32[1,128]{1,0:T(1,128)}) custom-call(f32[1,5,4,16,128]{4,3,2,1,0:T(8,128)} %get-tuple-element.22.left, f32[1,32]{1,0:T(1,128)} %get-tuple-element.23.coefs, f32[1,128]{1,0:T(1,128)} %get-tuple-element.24.square), custom_call_target="tpu_custom_call" | custom-call | tf_op jit(solution)/shard_map/cond/branch_1_fun/finish/pallas_call | solution.py:691

commit v3 on v2

--- a/solution.py
+++ b/solution.py
@@ -31,54 +31,63 @@
     return (blocks, krylov // blocks) if krylov % (8 * blocks) == 0 else (1, krylov)
 
 
-def stage(src, old, dst, snap, step, coupling, first_planes, planes, keep, gain):
-    rows, lanes = src.shape[2], src.shape[3]
+def stage(src, old, dst, rates, snap, step, coupling, lo, planes, keep, scale):
+    rows, lanes = snap.shape[3], snap.shape[4]
     row = lax.broadcasted_iota(jnp.int32, (rows, lanes), 0)
     top = row == 0
-    last = row == rows - 1
-    step_gain = time_step * gain
+    bottom = row == rows - 1
     mix = [[coupling[k, j] for j in range(5)] for k in range(5)]
-
-    def one_plane(p):
+    edge = viscosity * time_step
+
+    def cells(field, k, p, shift=0):
+        return field[k, pl.ds(p * rows + shift, rows)]
+
+    def make_rates(p):
         base = [snap[step, n, p].astype(f32) for n in range(4)]
-        half = [(0.5 * step_gain) * base[n] for n in range(3)]
-        edge = viscosity * step_gain
-        x_up, x_low = edge - half[0], edge + half[0]
-        y_up = jnp.where(last, 0.0, edge - half[1])
-        y_low = jnp.where(top, 0.0, edge + half[1])
-        z_up, z_low = edge - half[2], edge + half[2]
-        pull = step_gain * base[3]
-        center = [src[k, p] for k in range(5)]
-        own = gain - 6.0 * viscosity * step_gain
+        half = [(0.5 * time_step) * base[n] for n in range(3)]
+        pull = time_step * base[3]
+        found = [edge - half[0], edge + half[0]]
+        found += [jnp.where(bottom, 0.0, edge - half[1]), jnp.where(top, 0.0, edge + half[1])]
+        found += [edge - half[2], edge + half[2], pull]
+        own = 1.0 - 6.0 * edge
+        found += [own - pull * mix[k][k] for k in range(5)]
+        for n, rate in enumerate(found):
+            rates[step, n, p] = rate
+        return found
+
+    def body(i, carry):
+        p = lo + i
+        now = [rates[step, n, p] for n in range(12)] if keep else make_rates(p)
+        x_up, x_low, y_up, y_low, z_up, z_low, pull = now[:7]
+        center = [cells(src, k, p) for k in range(5)]
         for k in range(5):
             q = center[k]
-            coupled = mix[k][0] * center[0]
-            for j in range(1, 5):
+            others = [j for j in range(5) if j != k]
+            coupled = mix[k][others[0]] * center[others[0]]
+            for j in others[1:]:
                 coupled = coupled + mix[k][j] * center[j]
-            total = own * q - pull * coupled
-            total = total + (x_up * src[k, p + 1] + x_low * src[k, p - 1])
-            total = total + (y_up * pltpu.roll(q, rows - 1, 0) + y_low * pltpu.roll(q, 1, 0))
+            total = now[7 + k] * q - pull * coupled
+            total = total + (x_up * cells(src, k, p + 1) + x_low * cells(src, k, p - 1))
+            total = total + (y_up * cells(src, k, p, 1) + y_low * cells(src, k, p, -1))
             total = total + (z_up * pltpu.roll(q, lanes - 1, 1) + z_low * pltpu.roll(q, 1, 1))
             if keep:
-                total = total + keep * old[k, p]
-            dst[k, p] = total
-
-    def body(i, carry):
-        for lo in first_planes:
-            one_plane(lo + i)
+                total = total + keep * cells(old, k, p)
+            if scale != 1.0:
+                total = total * scale
+            dst[k, pl.ds(p * rows, rows)] = total
         return carry
 
-    unroll = max(n for n in range(1, 6) if planes % n == 0)
+    unroll = max(n for n in range(1, 5) if planes % n == 0)
     lax.fori_loop(0, planes, body, 0, unroll=unroll)
 
 
 def kernel(
     groups, tiles, coupling_in, basis, snapshots,
     left_out, coef_out, square_out, margin_out,
-    coupling, held, plain, start, snap, state, one, two, left, cross, rows_k, spread,
-    gram_send, gram_all, coef_send, coef_all, margin_send, margin_all, coefs, square_row, margin_row,
+    coupling, held, plain, start, snap, state, one, two, rates, cross, rows_k, spread,
+    gram_send, gram_all, coef_send, coef_all,
     load_sem, start_send, start_recv, snap_send, relay_send, snap_recv,
-    share_send, share_recv, margin_ssem, margin_rsem, out_sem, ready,
+    share_send, share_recv, pass_send, pass_recv, ready,
 ):
     g = lax.axis_index("grp")
     t = lax.axis_index("tile")
@@ -106,6 +115,8 @@
         return {"grp": lax.rem(g + other, groups), "tile": t}
 
     barrier = pltpu.get_barrier_semaphore()
+    reach = max(offsets)
+
     def crosses(d):
         return t + d >= tiles if d > 0 else t + d < 0
 
@@ -116,7 +127,12 @@
     for d in sorted(offsets, key=abs, reverse=True):
         if d > 0:
             greet(at(g, -d))
-            greeters = greeters + 1
+            greeters = greeters + 1 + jnp.where(crosses(d), groups - 1, 0)
+
+            @pl.when(crosses(-d))
+            def _():
+                for other in range(1, groups):
+                    greet(at(lax.rem(g + other, groups), -d))
         else:
             pl.when(jnp.logical_not(crosses(-d)))(functools.partial(greet, at(g, -d)))
             greeters = greeters + jnp.where(crosses(d), 0, 1)
@@ -186,6 +202,11 @@
                     for other in range(1 if d else groups):
                         if d or other:
                             act(snap_copy(s, inside[d], d, other))
+                    if d == reach:
+                        @pl.when(crosses(-d))
+                        def _():
+                            for other in range(1, groups):
+                                act(snap_copy(s, inside[d], d, other))
 
     def relay_copy(s, n, d, other):
         first, last = spans(slab, rim - 3 * s - 1)[d]
@@ -205,8 +226,15 @@
             for n, d in snap_offsets(s):
                 if d and d in ds:
                     snap_copy(s, n, d, 0).wait_recv()
-                    for other in range(1, groups):
-                        relay_copy(s, n, d, other).start()
+
+                    def forward():
+                        for other in range(1, groups):
+                            relay_copy(s, n, d, other).start()
+
+                    if d == reach:
+                        pl.when(jnp.logical_not(crosses(d)))(forward)
+                    else:
+                        forward()
             if 0 in ds:
                 local_snap(s).wait()
 
@@ -238,33 +266,65 @@
 
     for d in offsets:
         if d < 0:
-            pl.when(crosses(-d))(functools.partial(tell, edge - d - 1, at(g, -d)))
+            @pl.when(crosses(-d))
+            def _():
+                for other in range(groups):
+                    tell(edge - d - 1, at(lax.rem(g + other, groups), -d))
+
     upper = t >= tiles // 2
     ahead = [d for d in offsets if d < 0]
     back = [-d for d in ahead]
 
-    def send_near(s):
-        if s == 0:
-            snap_each(0, [0], lambda copy: copy.start())
-        else:
-            snap_each(s, [0], lambda copy: copy.start())
-        for d in sorted(offsets, key=abs):
+    def send_near(s, ds):
+        for d in ds:
             if d < 0:
                 send(s, [d])
             else:
                 pl.when(jnp.logical_not(crosses(-d)))(functools.partial(send, s, [d]))
 
+    def sided(act, *ds):
+        for way, on in ((1, upper), (-1, jnp.logical_not(upper))):
+            @pl.when(on)
+            def _():
+                act([way * d for d in ds])
+
+    near_ds, far_ds = sorted(ahead, key=abs), sorted(back)
+
+    turn = edge + len(back)
+
+    def wait_far(d):
+        pl.semaphore_wait(ready.at[edge + d - 1], groups)
+
+    def send_first():
+        wait_far(1)
+        one_start = start_copies[offsets.index(1)]
+        snap_each(0, [1], lambda copy: copy.start())
+        pl.when(g != 0)(one_start.start)
+        for s in range(1, steps):
+            send(s, [1])
+        for d in sorted(back)[1:]:
+            wait_far(d)
+            for s in range(steps):
+                send(s, [d])
+        pl.when(g == 0)(one_start.start)
+
     def send_late():
-        for d in sorted(back):
-            @pl.when(crosses(-d))
+        @pl.when((t > 0) & (t < reach))
+        def _():
+            pl.semaphore_wait(ready.at[turn], 1)
+
+        for d in sorted(back)[1:]:
+            @pl.when((t > 0) & crosses(-d))
             def _():
-                pl.semaphore_wait(ready.at[edge + d - 1], 1)
-                send(0, [d])
-                for s in range(1, steps):
+                wait_far(d)
+                for s in range(steps):
                     send(s, [d])
 
+        pl.when((t > 0) & (t + 1 < reach))(functools.partial(tell, turn, at(g, 1)))
+
     for s in range(steps):
-        send_near(s)
+        snap_each(s, [0], lambda copy: copy.start())
+        sided(functools.partial(send_near, s), *near_ds, *far_ds)
 
     def flip_step(n):
         if n:
@@ -297,67 +357,86 @@
         for other in range(1, groups):
             tell(len(levels) + 2, partner(other))
 
-    pending = [functools.partial(flip_step, n) for n in range(len(levels) + 1)]
-    pending += [functools.partial(chain_step, n) for n in range(2)] + [tell_group]
-
-    def advance():
-        if pending:
-            pl.when(g == groups - 1)(pending.pop(0))
-
-    def all_ready():
-        while pending:
-            advance()
-        if groups > 1:
-            @pl.when(g != groups - 1)
-            def _():
-                pl.semaphore_wait(ready.at[len(levels) + 2], 1)
-
-    advance()
     pltpu.make_async_copy(basis, held, load_sem.at[2]).wait()
+
+    def expand(k, carry):
+        plain[k] = held[k].astype(f32)
+        return carry
+
+    lax.fori_loop(0, krylov, expand, 0)
     size = krylov * ny
-    for c in range(parts):
-        wide = jnp.concatenate([held[:, c, x].reshape(size, nz) for x in range(slab)], axis=1)
-        piece = lax.dot_general(wide, wide, (((1,), (1,)), ((), ())), preferred_element_type=f32)
-        cross[...] = cross[...] + piece if c else piece
-        if c == min(3, parts - 1):
-            send_late()
-        advance()
-    line = lax.broadcasted_iota(jnp.int32, (size, size), 0)
-    column = lax.broadcasted_iota(jnp.int32, (size, size), 1)
-    kept = jnp.where(lax.rem(line, ny) == lax.rem(column, ny), cross[...], 0.0)
-    kept = jnp.sum(kept.reshape(krylov, ny, size), axis=1)
-    pick = (
-        lax.broadcasted_iota(jnp.int32, (size, krylov), 0) // ny
-        == lax.broadcasted_iota(jnp.int32, (size, krylov), 1)
-    ).astype(f32)
-    gram = jnp.dot(kept, pick, precision=HIGHEST, preferred_element_type=f32)
     blocks, height = gram_blocks(krylov, nz)
-    gram_send[...] = jnp.concatenate(
-        [gram[n * height : (n + 1) * height] for n in range(blocks)], axis=1
-    )
-    def spread_out(n, send, everyone):
+
+    def gram_copy(other):
+        return pltpu.make_async_remote_copy(
+            src_ref=gram_send,
+            dst_ref=gram_send,
+            send_sem=pass_send.at[other],
+            recv_sem=pass_recv.at[0],
+            device_id=partner(other),
+            device_id_type=MESH,
+        )
+
+    @pl.when(g == 0)
+    def _():
+        for c in range(parts):
+            wide = jnp.concatenate([held[:, c, x].reshape(size, nz) for x in range(slab)], axis=1)
+            piece = lax.dot_general(wide, wide, (((1,), (1,)), ((), ())), preferred_element_type=f32)
+            cross[...] = cross[...] + piece if c else piece
+        line = lax.broadcasted_iota(jnp.int32, (size, size), 0)
+        column = lax.broadcasted_iota(jnp.int32, (size, size), 1)
+        kept = jnp.where(lax.rem(line, ny) == lax.rem(column, ny), cross[...], 0.0)
+        kept = jnp.sum(kept.reshape(krylov, ny, size), axis=1)
+        pick = (
+            lax.broadcasted_iota(jnp.int32, (size, krylov), 0) // ny
+            == lax.broadcasted_iota(jnp.int32, (size, krylov), 1)
+        ).astype(f32)
+        gram = jnp.dot(kept, pick, precision=HIGHEST, preferred_element_type=f32)
+        gram_send[...] = jnp.concatenate(
+            [gram[n * height : (n + 1) * height] for n in range(blocks)], axis=1
+        )
+        for other in range(1, groups):
+            gram_copy(other).start()
+
+    @pl.when(g == groups - 1)
+    def _():
+        for n in range(len(levels) + 1):
+            flip_step(n)
+        chain_step(0)
+
+    pl.when(t == 0)(send_first)
+    @pl.when(g == groups - 1)
+    def _():
+        chain_step(1)
+        for other in range(1, groups):
+            tell(len(levels) + 2, partner(other))
+
+    def spread_out(n, send, everyone, reached):
         way = 2 * (t // max(tiles // 2, 1)) - 1
-        others = everyone.at[pl.ds(0, tiles - 1)]
+        others = everyone.at[pl.ds(0, reached * tiles - 1)]
+        place = t if reached == 1 else g * tiles + t
 
         def begin():
             def one(i, carry):
                 peer = lax.rem(2 * tiles - 1 - t + way * i, tiles)
 
-                @pl.when(peer != t)
-                def _():
+                def to(other):
                     pltpu.make_async_remote_copy(
                         src_ref=send,
-                        dst_ref=everyone.at[t],
+                        dst_ref=everyone.at[place],
                         send_sem=share_send.at[n],
                         recv_sem=share_recv.at[n],
-                        device_id={"grp": g, "tile": peer},
+                        device_id={"grp": lax.rem(g + other, groups), "tile": peer},
                         device_id_type=MESH,
                     ).start()
 
+                pl.when(peer != t)(functools.partial(to, 0))
+                for other in range(1, reached):
+                    to(other)
                 return carry
 
             lax.fori_loop(0, tiles, one, 0)
-            everyone[t] = send[...]
+            everyone[place] = send[...]
 
         def arrive():
             pltpu.make_async_copy(others, others, share_recv.at[n]).wait()
@@ -367,19 +446,12 @@
 
         return begin, arrive, drain
 
-    gram_begin, gram_arrive, gram_drain = spread_out(0, gram_send, gram_all)
-    coef_begin, coef_arrive, coef_drain = spread_out(1, coef_send, coef_all)
-
-    def expand(k, carry):
-        plain[k] = held[k].astype(f32)
-        return carry
-
-    lax.fori_loop(0, krylov, expand, 0)
-
+    gram_begin, gram_arrive, gram_drain = spread_out(0, gram_send, gram_all, 1)
+    coef_begin, coef_arrive, coef_drain = spread_out(1, coef_send, coef_all, groups)
     def widen(d):
         def one(p, carry):
             for k in range(parts):
-                state[k, p] = start[k, p].astype(f32)
+                state[k, pl.ds(p * ny, ny)] = start[k, p].astype(f32)
             return carry
 
         lo, width = (rim, slab) if d == 0 else (rim + d * slab + near[d][0], near[d][1] - near[d][0])
@@ -394,7 +466,7 @@
                 mix.wait()
             widen(d)
 
-    weights = ((0.0, 1.0), (0.75, 0.25), (1.0 / 3.0, 2.0 / 3.0))
+    keeps = (0.0, 3.0, 2.0)
     ways = ((state, one), (one, two), (two, state))
 
     def march(s, known, new):
@@ -403,35 +475,61 @@
             lo, hi = max(k, known - k), new - k
             if hi > lo:
                 first = jnp.where(upper, lo, planes - hi)
-                stage(src, state, dst, snap, s, coupling, [first], hi - lo, *weights[n])
-
-    def sided(act, *ds):
+                scale = 6.0 ** -steps if k == 3 * steps else 1.0
+                stage(src, state, dst, rates, snap, s, coupling, first, hi - lo, keeps[n], scale)
+
+    def relay_far(s, d, early):
         for way, on in ((1, upper), (-1, jnp.logical_not(upper))):
-            @pl.when(on)
+            seam = crosses(way * d)
+
+            @pl.when(on & (jnp.logical_not(seam) if early else seam))
             def _():
-                act([way * d for d in ds])
-
-    near_ds, far_ds = sorted(ahead, key=abs), sorted(back)
-    sided(lambda ds: (relay(0, [0] + ds), arrive(ds)), *near_ds)
+                relay(s, [way * d])
+
+    sided(lambda ds: relay(0, [0] + ds), *near_ds)
+    sided(arrive, *near_ds)
     arrive([0])
     for s in range(1, steps):
         sided(lambda ds: relay(s, [0] + ds), *near_ds)
+    relay_far(0, far_ds[0], True)
     sided(lambda ds: receive(0, [0] + ds), *near_ds)
+    if reach > 1:
+        pl.when(t == 0)(functools.partial(tell, turn, at(g, 1)))
     known = 0
     for piece in range(len(far_ds) + 1):
         if piece:
-            sided(lambda ds: (relay(0, ds), arrive(ds)), far_ds[piece - 1])
+            d = far_ds[piece - 1]
+            if piece == 1:
+                relay_far(0, d, False)
+            sided(arrive, d)
             for s in range(1, steps):
-                sided(lambda ds: relay(s, ds), far_ds[piece - 1])
-            sided(lambda ds: receive(0, ds), far_ds[piece - 1])
+                relay_far(s, d, False)
+            sided(lambda ds: receive(0, ds), d)
         new = rim + slab + sum(near[d][1] - near[d][0] for d in far_ds[:piece])
         for s in range(steps):
             if s:
                 sided(lambda ds: receive(s, ds), *(([0] + near_ds) if piece == 0 else far_ds[piece - 1 : piece]))
             march(s, known, new)
+            if piece and s == 0 and piece < len(far_ds):
+                relay_far(0, far_ds[piece], False)
+            if piece == 0 and s == 0:
+                send_late()
+                for d in far_ds[1:]:
+                    relay_far(0, d, True)
+                for later in range(1, steps):
+                    for d in far_ds:
+                        relay_far(later, d, True)
         known = new
         if piece == 0:
-            all_ready()
+            if groups > 1:
+                @pl.when(g != groups - 1)
+                def _():
+                    pl.semaphore_wait(ready.at[len(levels) + 2], 1)
+
+                @pl.when(g != 0)
+                def _():
+                    gram_copy(0).wait_recv()
+
             gram_begin()
 
     count = f32(parts * slab * ny * nz * tiles)
@@ -442,7 +540,7 @@
         totals = [jnp.zeros((ny, nz), f32) for _ in range(group)]
         for c in range(parts):
             for x in range(slab):
-                field = state[c, rim + x]
+                field = state[c, pl.ds((rim + x) * ny, ny)]
                 for n in range(group):
                     totals[n] = totals[n] + plain[i * group + n, c, x] * field
         for n in range(group):
@@ -457,7 +555,7 @@
     own_square = jnp.zeros((ny, nz), f32)
     for c in range(parts):
         for x in range(slab):
-            own_square = own_square + state[c, rim + x] * state[c, rim + x]
+            own_square = own_square + state[c, pl.ds((rim + x) * ny, ny)] * state[c, pl.ds((rim + x) * ny, ny)]
     own_square = jnp.sum(jnp.sum(own_square, axis=0, keepdims=True), axis=1, keepdims=True)
     coef_send[...] = jnp.concatenate(
         [inner[0:1], jnp.broadcast_to(own_square, (1, coef_send.shape[1] - krylov))], axis=1
@@ -473,11 +571,27 @@
         @pl.when(g == s // local)
         def _():
             all_sent(snap.at[s, :, pl.ds(0, around)], snap_send.at[s % local])
+            last = spans(slab, rim - 3 * s - 1).get(reach, (0, 0))
+            last = last[1] - last[0]
             for other in range(1, groups):
                 all_sent(snap.at[s, :, pl.ds(0, slab)], snap_send.at[s % local])
-                all_sent(snap.at[s, :, pl.ds(0, around)], relay_send.at[s % local])
+                all_sent(snap.at[s, :, pl.ds(0, around - last)], relay_send.at[s % local])
+                if last:
+                    @pl.when(crosses(-reach))
+                    def _():
+                        all_sent(snap.at[s, :, pl.ds(0, last)], snap_send.at[s % local])
+
+                    @pl.when(jnp.logical_not(crosses(reach)))
+                    def _():
+                        all_sent(snap.at[s, :, pl.ds(0, last)], relay_send.at[s % local])
 
     gram_drain()
+
+    @pl.when(g == 0)
+    def _():
+        for other in range(1, groups):
+            gram_copy(other).wait_send()
+
     gram_arrive()
     packed = jnp.sum(gram_all[...], axis=0) / count
     gram = jnp.concatenate(
@@ -487,45 +601,27 @@
     times = functools.partial(jnp.dot, precision=HIGHEST, preferred_element_type=f32)
     twice = jnp.where(same, 2.0, 0.0) - gram
     both = jnp.concatenate([twice, times(twice, gram)], axis=1)
+    reach_row = jnp.sum(jnp.abs(gram), axis=0, keepdims=True)
     coef_arrive()
-    sums = jnp.sum(coef_all[...], axis=0) / count
-    first_row = jnp.broadcast_to(sums, (8, sums.shape[1]))
-    work_square = first_row[:, krylov : krylov + 1]
-    first_row = first_row[:, :krylov]
-    mixed = times(first_row, both)
+    sums = [jnp.sum(coef_all[n * tiles : (n + 1) * tiles], axis=0) / count for n in range(groups)]
+    sums = jnp.concatenate(sums + [jnp.zeros((-groups % 8, sums[0].shape[1]), f32)], axis=0)
+    first_rows, work_square = sums[:, :krylov], sums[:, krylov : krylov + 1]
+    mixed = times(first_rows, both)
     every, turned = mixed[:, :krylov], mixed[:, krylov:]
+    group_row = lax.broadcasted_iota(jnp.int32, work_square.shape, 0)
+    own_every = jnp.sum(jnp.where(group_row == g, every, 0.0), axis=0, keepdims=True)
     for k in range(krylov):
-        spread[k] = jnp.broadcast_to(every[:, k : k + 1], (8, nz))
-    linear = 2.0 * every * first_row
+        spread[k] = jnp.broadcast_to(own_every[:, k : k + 1], (8, nz))
+    linear = 2.0 * every * first_rows
     bent = every * turned
-    bound = 2.0 * jnp.abs(every * first_row) + jnp.abs(every) * times(jnp.abs(every), jnp.abs(gram))
+    bound = jnp.abs(linear) + every * every * reach_row
     square = work_square + jnp.sum(bent - linear, axis=1, keepdims=True)
     bound = work_square + jnp.sum(bound, axis=1, keepdims=True)
-    margin = square - cancel_limit * bound
-    margin_send[...] = jnp.broadcast_to(margin[0:1], margin_send.shape)
-
-    def margin_copy(other, sender):
-        return pltpu.make_async_remote_copy(
-            src_ref=margin_send,
-            dst_ref=margin_all.at[sender],
-            send_sem=margin_ssem.at[other],
-            recv_sem=margin_rsem.at[other],
-            device_id=partner(other),
-            device_id_type=MESH,
-        )
-
-    for other in range(1, groups):
-        margin_copy(other, g).start()
-    margin_all[g] = margin_send[...]
-
-    square_row[...] = jnp.broadcast_to(square[0:1], square_row.shape)
-    coefs[...] = every[0:1]
-    outs = [
-        pltpu.make_async_copy(coefs, coef_out, out_sem.at[0]),
-        pltpu.make_async_copy(square_row, square_out, out_sem.at[1]),
-    ]
-    for copy in outs:
-        copy.start()
+    margin = jnp.where(group_row < groups, square - cancel_limit * bound, jnp.inf)
+    margin_out[...] = jnp.broadcast_to(jnp.min(margin, axis=0, keepdims=True), margin_out.shape)
+    square = jnp.sum(jnp.where(group_row == g, square, 0.0), axis=0, keepdims=True)
+    square_out[...] = jnp.broadcast_to(square, square_out.shape)
+    coef_out[...] = own_every
     for x in range(slab):
         removed = [jnp.zeros((ny // 8, 8, nz), f32) for _ in range(parts)]
         for k in range(krylov):
@@ -533,21 +629,8 @@
             for c in range(parts):
                 removed[c] = removed[c] + factor * plain[k, c, x].reshape(ny // 8, 8, nz)
         for c in range(parts):
-            left[c, x] = state[c, rim + x] - removed[c].reshape(ny, nz)
-        copy = pltpu.make_async_copy(left.at[:, x], left_out.at[0, :, x], out_sem.at[3])
-        copy.start()
-    for other in range(1, groups):
-        margin_copy(other, lax.rem(g - other + groups, groups)).wait_recv()
-    margin_row[...] = jnp.min(margin_all[...], axis=0)
-    copy = pltpu.make_async_copy(margin_row, margin_out, out_sem.at[2])
-    copy.start()
-    outs.append(copy)
+            left_out[0, c, x] = state[c, pl.ds((rim + x) * ny, ny)] - removed[c].reshape(ny, nz)
     coef_drain()
-    for other in range(1, groups):
-        margin_copy(other, g).wait_send()
-    for copy in outs:
-        copy.wait()
-    pltpu.make_async_copy(left, left_out.at[0], out_sem.at[3]).wait()
 
 
 def square_kernel(tiles, left, square_out, send, everyone, ssem, rsem):
@@ -592,34 +675,22 @@
     lax.fori_loop(1, tiles, lambda r, c: (copy(r, t).wait_send(), c)[1], 0)
 
 
-def finish(left, coefs, square, out, coef_out, norm_out, held, row, norm_row, line, sem):
-    loads = [
-        pltpu.make_async_copy(square, row, sem.at[0]),
-        pltpu.make_async_copy(left, held, sem.at[1]),
-        pltpu.make_async_copy(coefs, line, sem.at[2]),
+def finish(left, coefs, square, out, coef_out, norm_out, held, norm_row, sem):
+    norm = jnp.sqrt(square[...])
+    norm_row[...] = norm
+    inverse = jnp.broadcast_to(1.0 / norm, left.shape[3:])
+    copies = [
+        pltpu.make_async_copy(norm_row, norm_out, sem.at[0]),
+        pltpu.make_async_copy(coefs, coef_out, sem.at[1]),
     ]
-    for copy in loads:
-        copy.start()
-    loads[0].wait()
-    norm = jnp.sqrt(row[...])
-    norm_row[...] = norm
-    loads[2].wait()
-    stores = [
-        pltpu.make_async_copy(norm_row, norm_out, sem.at[0]),
-        pltpu.make_async_copy(line, coef_out, sem.at[2]),
-    ]
-    for copy in stores:
-        copy.start()
-    inverse = jnp.broadcast_to(1.0 / norm, left.shape[3:])
-    loads[1].wait()
     for c in range(left.shape[1]):
         for x in range(left.shape[2]):
-            held[0, c, x] = held[0, c, x] * inverse
-    last = pltpu.make_async_copy(held, out, sem.at[1])
-    last.start()
-    for copy in stores:
+            held[0, c, x] = left[0, c, x] * inverse
+    copies.append(pltpu.make_async_copy(held, out, sem.at[2]))
+    for copy in copies:
+        copy.start()
+    for copy in copies:
         copy.wait()
-    last.wait()
 
 
 def on_device(groups, tiles, basis, snapshots, coupling):
@@ -632,9 +703,9 @@
     blocks, height = gram_blocks(krylov, nz)
     width = -(-(krylov + 1) // nz) * nz
     dma = pltpu.SemaphoreType.DMA
-    field = pltpu.VMEM((parts, planes, ny, nz), f32)
+    field = pltpu.VMEM((parts, planes * ny, nz), f32)
     whole = pl.BlockSpec(memory_space=pltpu.VMEM)
-    anywhere = pl.BlockSpec(memory_space=pl.ANY)
+    outside = pl.BlockSpec(memory_space=pltpu.HBM)
     results = pl.pallas_call(
         functools.partial(kernel, groups, tiles),
         name="propagate",
@@ -644,8 +715,8 @@
             jax.ShapeDtypeStruct((1, nz), f32),
             jax.ShapeDtypeStruct((1, nz), f32),
         ),
-        in_specs=[anywhere] * 3,
-        out_specs=(anywhere,) * 4,
+        in_specs=[outside] * 3,
+        out_specs=(whole,) * 4,
         scratch_shapes=[
             pltpu.SMEM(coupling.shape, f32),
             pltpu.VMEM(basis.shape, bf16),
@@ -655,19 +726,14 @@
             field,
             field,
             field,
-            pltpu.VMEM((parts, slab, ny, nz), f32),
+            pltpu.VMEM((steps, 12, planes, ny, nz), f32),
             pltpu.VMEM((krylov * ny, krylov * ny), f32),
             pltpu.VMEM((krylov, nz), f32),
             pltpu.VMEM((krylov, 8, nz), f32),
             pltpu.VMEM((height, blocks * krylov), f32),
             pltpu.VMEM((tiles, height, blocks * krylov), f32),
             pltpu.VMEM((1, width), f32),
-            pltpu.VMEM((tiles, 1, width), f32),
-            pltpu.VMEM((1, nz), f32),
-            pltpu.VMEM((groups, 1, nz), f32),
-            pltpu.VMEM((1, krylov), f32),
-            pltpu.VMEM((1, nz), f32),
-            pltpu.VMEM((1, nz), f32),
+            pltpu.VMEM((groups * tiles, 1, width), f32),
             dma((3 + local,)),
             dma((1,)),
             dma((count,)),
@@ -677,14 +743,13 @@
             dma((2,)),
             dma((2,)),
             dma((groups,)),
-            dma((groups,)),
-            dma((4,)),
-            pltpu.SemaphoreType.REGULAR((tiles.bit_length() + 2 + -(-rim // slab),)),
+            dma((1,)),
+            pltpu.SemaphoreType.REGULAR((tiles.bit_length() + 3 + -(-rim // slab),)),
         ],
         compiler_params=pltpu.CompilerParams(
-            collective_id=0, has_side_effects=True, vmem_limit_bytes=67043328
+            collective_id=0, has_side_effects=True, vmem_limit_bytes=48 << 20
         ),
-    )(coupling, basis, snapshots)
+    )(*(pltpu.with_memory_space_constraint(a, pltpu.HBM) for a in (coupling, basis, snapshots)))
     left, coefs, square, margin = results
 
     def scaled(left, coefs, square):
@@ -692,13 +757,11 @@
             finish,
             name="finish",
             out_shape=tuple(jax.ShapeDtypeStruct(a.shape, f32) for a in (left, coefs, square)),
-            in_specs=[anywhere] * 3,
-            out_specs=(anywhere,) * 3,
+            in_specs=[whole] * 3,
+            out_specs=(outside,) * 3,
             scratch_shapes=[
                 pltpu.VMEM(left.shape, f32),
                 pltpu.VMEM(square.shape, f32),
-                pltpu.VMEM(square.shape, f32),
-                pltpu.VMEM(coefs.shape, f32),
                 dma((3,)),
             ],
         )(left, coefs, square)

time: 26.8 us -> 26.2 us (0.978)
  between operations: 1.27 us -> 0.67 us
    pallas_call x1, Pallas kernels: 1.62 us -> 0.72 us  [scaled(): pl.pallas_call(finish, name='finish', out_shape=tuple((jax.ShapeDtypeStru...]
    pallas_call x1, Pallas kernels: 23.7 us -> 24.6 us  [on_device(): pl.pallas_call(functools.partial(kernel, groups, tiles), name='propagate'...]
where the time goes in v3:
time: 26.2 us; the launch traced here: 26 us
  Pallas kernels  25.3 us (97%)
  between operations  0.67 us (3%)
    pallas_call x1, Pallas kernels, on_device(): pl.pallas_call(functools.partial(kernel, groups, tiles), name='propagate'...  24.6 us
    pallas_call x1, Pallas kernels, scaled(): pl.pallas_call(finish, name='finish', out_shape=tuple((jax.ShapeDtypeStru...  0.72 us

profile of v3, /device:TPU:0, one launch (start us, length us, event | category | flops | bytes accessed | tf_op | source)
XLA Modules:
  0.0 26.0 jit_solution(15482973995422835481)
XLA Ops:
  0.6 24.6 %propagate.1 = (f32[1,5,4,16,128]{4,3,2,1,0:T(8,128)S(1)}, f32[1,32]{1,0:T(1,128)S(1)}, f32[1,128]{1,0:T(1,128)S(1)}, f32[1,128]{1,0:T(1,128)S(1)}) custom-call(f32[5,5]{1,0:T(8,128)} %coupling_in.1, bf16[32,5,4,16,128]{4,3,2,1,0:T(8,128)(2,1)} %basis.1, bf16[1,4,4,16,128]{4,3,2,1,0:T(8,128)(2,1)} %snapshots.1), custom_call_target="tpu_custom_call" | custom-call | tf_op jit(solution)/shard_map/propagate/pallas_call | solution.py:709
  25.3 0.7 %conditional.1 = (f32[1,5,4,16,128]{4,3,2,1,0:T(8,128)}, f32[1,32]{1,0:T(1,128)}, f32[1]{0:T(128)}) conditional(s32[]{:T(128)} %bitcast.2, (f32[1,5,4,16,128]{4,3,2,1,0:T(8,128)S(1)}, f32[1,32]{1,0:T(1,128)S(1)}) %tuple.17, (f32[1,5,4,16,128]{4,3,2,1,0:T(8,128)S(1)}, f32[1,32]{1,0:T(1,128)S(1)}, f32[1,128]{1,0:T(1,128)S(1)}) %tuple.18), branch_computations={%region_0.0_spmd, %region_1.0_spmd} | conditional | bytes 24 | solution.py:786
  25.3 0.7 %finish.3 = (f32[1,5,4,16,128]{4,3,2,1,0:T(8,128)}, f32[1,32]{1,0:T(1,128)}, f32[1,128]{1,0:T(1,128)}) custom-call(f32[1,5,4,16,128]{4,3,2,1,0:T(8,128)S(1)} %get-tuple-element.22.left, f32[1,32]{1,0:T(1,128)S(1)} %get-tuple-element.23.coefs, f32[1,128]{1,0:T(1,128)S(1)} %get-tuple-element.24.square), custom_call_target="tpu_custom_call" | custom-call | tf_op jit(solution)/shard_map/cond/branch_1_fun/finish/pallas_call | solution.py:756

commit v4 on v3

--- a/solution.py
+++ b/solution.py
@@ -136,6 +136,11 @@
         else:
             pl.when(jnp.logical_not(crosses(-d)))(functools.partial(greet, at(g, -d)))
             greeters = greeters + jnp.where(crosses(d), 0, 1)
+    held_back = near[reach][1] - near[reach][0]
+    carried = reach > 1 and held_back < slab and 2 * reach < tiles
+    if carried:
+        pl.when(t == reach)(functools.partial(greet, {"grp": g, "tile": tiles - 1}))
+        greeters = greeters + jnp.where(t == tiles - 1, 1, 0)
     for other in range(1, groups):
         greet(partner(other))
     for way in (1, -1):
@@ -291,36 +296,58 @@
     near_ds, far_ds = sorted(ahead, key=abs), sorted(back)
 
     turn = edge + len(back)
+    if carried:
+        pl.when(t == tiles - 1)(functools.partial(tell, turn, {"grp": g, "tile": reach}))
 
     def wait_far(d):
         pl.semaphore_wait(ready.at[edge + d - 1], groups)
 
+    def start_copy(d, group, last):
+        first = near[d][0]
+        return pltpu.make_async_remote_copy(
+            src_ref=basis.at[krylov - groups + group, :, pl.ds(first, last - first)],
+            dst_ref=start.at[:, target(d, first, last)],
+            send_sem=start_send.at[0],
+            recv_sem=start_recv.at[offsets.index(d)],
+            device_id=at(group, -d),
+            device_id_type=MESH,
+        )
+
     def send_first():
         wait_far(1)
-        one_start = start_copies[offsets.index(1)]
         snap_each(0, [1], lambda copy: copy.start())
-        pl.when(g != 0)(one_start.start)
+        start_copy(1, g, slab - held_back if carried else slab).start()
         for s in range(1, steps):
             send(s, [1])
         for d in sorted(back)[1:]:
             wait_far(d)
             for s in range(steps):
-                send(s, [d])
-        pl.when(g == 0)(one_start.start)
+                snap_each(s, [d], lambda copy: copy.start())
+
+    def send_second():
+        for d in sorted(back)[1:]:
+            for group in range(groups):
+                start_copy(d, group, near[d][1]).start()
+
+    def send_carried():
+        start_copies[offsets.index(-reach)].wait_recv()
+        pl.semaphore_wait(ready.at[turn], 1)
+        pltpu.make_async_remote_copy(
+            src_ref=start.at[:, target(-reach, slab - held_back, slab)],
+            dst_ref=start.at[:, target(1, slab - held_back, slab)],
+            send_sem=start_send.at[0],
+            recv_sem=start_recv.at[offsets.index(1)],
+            device_id={"grp": g, "tile": tiles - 1},
+            device_id_type=MESH,
+        ).start()
 
     def send_late():
-        @pl.when((t > 0) & (t < reach))
-        def _():
-            pl.semaphore_wait(ready.at[turn], 1)
-
         for d in sorted(back)[1:]:
             @pl.when((t > 0) & crosses(-d))
             def _():
                 wait_far(d)
                 for s in range(steps):
                     send(s, [d])
-
-        pl.when((t > 0) & (t + 1 < reach))(functools.partial(tell, turn, at(g, 1)))
 
     for s in range(steps):
         snap_each(s, [0], lambda copy: copy.start())
@@ -405,6 +432,9 @@
         chain_step(0)
 
     pl.when(t == 0)(send_first)
+    send_late()
+    if carried:
+        pl.when(t == reach)(send_carried)
     @pl.when(g == groups - 1)
     def _():
         chain_step(1)
@@ -459,7 +489,9 @@
 
     def arrive(ds):
         for d in ds:
-            if d:
+            if d == -reach and carried:
+                pl.when(t != reach)(start_copies[offsets.index(d)].wait_recv)
+            elif d:
                 start_copies[offsets.index(d)].wait_recv()
             else:
                 own.wait()
@@ -493,8 +525,7 @@
         sided(lambda ds: relay(s, [0] + ds), *near_ds)
     relay_far(0, far_ds[0], True)
     sided(lambda ds: receive(0, [0] + ds), *near_ds)
-    if reach > 1:
-        pl.when(t == 0)(functools.partial(tell, turn, at(g, 1)))
+    pl.when((t == 0) & (g == groups - 1))(send_second)
     known = 0
     for piece in range(len(far_ds) + 1):
         if piece:
@@ -513,7 +544,6 @@
             if piece and s == 0 and piece < len(far_ds):
                 relay_far(0, far_ds[piece], False)
             if piece == 0 and s == 0:
-                send_late()
                 for d in far_ds[1:]:
                     relay_far(0, d, True)
                 for later in range(1, steps):
@@ -564,7 +594,24 @@
     def all_sent(cells, sem):
         pltpu.make_async_copy(cells, cells, sem).wait()
 
-    all_sent(start.at[:, pl.ds(0, 2 * rim)], start_send.at[0])
+    moved = sum(near[d][1] - near[d][0] for d in sorted(back)[1:])
+    spare = held_back if carried else 0
+    all_sent(start.at[:, pl.ds(0, 2 * rim - moved - spare)], start_send.at[0])
+    if moved + spare:
+        @pl.when(t > 0)
+        def _():
+            all_sent(start.at[:, pl.ds(0, moved + spare)], start_send.at[0])
+
+        @pl.when((t == 0) & (g == groups - 1))
+        def _():
+            for _ in range(groups):
+                all_sent(start.at[:, pl.ds(0, moved)], start_send.at[0])
+
+    if spare:
+        @pl.when(t == reach)
+        def _():
+            all_sent(start.at[:, pl.ds(0, spare)], start_send.at[0])
+
     for s in range(steps):
         around = 2 * (rim - 3 * s - 1)
 

time: 26.2 us -> 23.4 us (0.89)
  Pallas kernels: 25.3 us -> 22.6 us
    pallas_call x1, Pallas kernels: 24.6 us -> 21.8 us  [on_device(): pl.pallas_call(functools.partial(kernel, groups, tiles), name='propagate'...]
where the time goes in v4:
time: 23.4 us; the launch traced here: 23.2 us
  Pallas kernels  22.6 us (97%)
  between operations  0.67 us (3%)
    pallas_call x1, Pallas kernels, on_device(): pl.pallas_call(functools.partial(kernel, groups, tiles), name='propagate'...  21.8 us
    pallas_call x1, Pallas kernels, scaled(): pl.pallas_call(finish, name='finish', out_shape=tuple((jax.ShapeDtypeStru...  0.72 us

profile of v4, /device:TPU:0, one launch (start us, length us, event | category | flops | bytes accessed | tf_op | source)
XLA Modules:
  0.0 23.2 jit_solution(6101543384196366103)
XLA Ops:
  0.6 21.8 %propagate.1 = (f32[1,5,4,16,128]{4,3,2,1,0:T(8,128)S(1)}, f32[1,32]{1,0:T(1,128)S(1)}, f32[1,128]{1,0:T(1,128)S(1)}, f32[1,128]{1,0:T(1,128)S(1)}) custom-call(f32[5,5]{1,0:T(8,128)} %coupling_in.1, bf16[32,5,4,16,128]{4,3,2,1,0:T(8,128)(2,1)} %basis.1, bf16[1,4,4,16,128]{4,3,2,1,0:T(8,128)(2,1)} %snapshots.1), custom_call_target="tpu_custom_call" | custom-call | tf_op jit(solution)/shard_map/propagate/pallas_call | solution.py:756
  22.5 0.7 %conditional.1 = (f32[1,5,4,16,128]{4,3,2,1,0:T(8,128)}, f32[1,32]{1,0:T(1,128)}, f32[1]{0:T(128)}) conditional(s32[]{:T(128)} %bitcast.2, (f32[1,5,4,16,128]{4,3,2,1,0:T(8,128)S(1)}, f32[1,32]{1,0:T(1,128)S(1)}) %tuple.17, (f32[1,5,4,16,128]{4,3,2,1,0:T(8,128)S(1)}, f32[1,32]{1,0:T(1,128)S(1)}, f32[1,128]{1,0:T(1,128)S(1)}) %tuple.18), branch_computations={%region_0.0_spmd, %region_1.0_spmd} | conditional | bytes 24 | solution.py:833
  22.5 0.7 %finish.3 = (f32[1,5,4,16,128]{4,3,2,1,0:T(8,128)}, f32[1,32]{1,0:T(1,128)}, f32[1,128]{1,0:T(1,128)}) custom-call(f32[1,5,4,16,128]{4,3,2,1,0:T(8,128)S(1)} %get-tuple-element.22.left, f32[1,32]{1,0:T(1,128)S(1)} %get-tuple-element.23.coefs, f32[1,128]{1,0:T(1,128)S(1)} %get-tuple-element.24.square), custom_call_target="tpu_custom_call" | custom-call | tf_op jit(solution)/shard_map/cond/branch_1_fun/finish/pallas_call | solution.py:803

commit v5 on v4

--- a/solution.py
+++ b/solution.py
@@ -280,12 +280,13 @@
     ahead = [d for d in offsets if d < 0]
     back = [-d for d in ahead]
 
-    def send_near(s, ds):
-        for d in ds:
-            if d < 0:
-                send(s, [d])
-            else:
-                pl.when(jnp.logical_not(crosses(-d)))(functools.partial(send, s, [d]))
+    def send_some(s, soon):
+        for d in sorted(offsets, key=abs):
+            wanted = t - d >= tiles // 2 if d < 0 else t - d < tiles // 2
+            wanted = wanted if soon else jnp.logical_not(wanted)
+            if d > 0:
+                wanted = wanted & jnp.logical_not(crosses(-d))
+            pl.when(wanted)(functools.partial(send, s, [d]))
 
     def sided(act, *ds):
         for way, on in ((1, upper), (-1, jnp.logical_not(upper))):
@@ -351,7 +352,13 @@
 
     for s in range(steps):
         snap_each(s, [0], lambda copy: copy.start())
-        sided(functools.partial(send_near, s), *near_ds, *far_ds)
+        send_some(s, True)
+
+    def send_far():
+        for s in range(steps):
+            send_some(s, False)
+
+    pl.when(t == 0)(send_far)
 
     def flip_step(n):
         if n:
@@ -410,6 +417,8 @@
             wide = jnp.concatenate([held[:, c, x].reshape(size, nz) for x in range(slab)], axis=1)
             piece = lax.dot_general(wide, wide, (((1,), (1,)), ((), ())), preferred_element_type=f32)
             cross[...] = cross[...] + piece if c else piece
+            if c == parts // 2:
+                pl.when(t > 0)(send_far)
         line = lax.broadcasted_iota(jnp.int32, (size, size), 0)
         column = lax.broadcasted_iota(jnp.int32, (size, size), 1)
         kept = jnp.where(lax.rem(line, ny) == lax.rem(column, ny), cross[...], 0.0)
@@ -429,6 +438,11 @@
     def _():
         for n in range(len(levels) + 1):
             flip_step(n)
+
+    pl.when((t > 0) & (g != 0))(send_far)
+
+    @pl.when(g == groups - 1)
+    def _():
         chain_step(0)
 
     pl.when(t == 0)(send_first)
@@ -523,34 +537,31 @@
     arrive([0])
     for s in range(1, steps):
         sided(lambda ds: relay(s, [0] + ds), *near_ds)
-    relay_far(0, far_ds[0], True)
     sided(lambda ds: receive(0, [0] + ds), *near_ds)
     pl.when((t == 0) & (g == groups - 1))(send_second)
     known = 0
-    for piece in range(len(far_ds) + 1):
-        if piece:
-            d = far_ds[piece - 1]
-            if piece == 1:
+    for far in (False, True):
+        if far:
+            for d in far_ds:
                 relay_far(0, d, False)
-            sided(arrive, d)
+            sided(arrive, *far_ds)
             for s in range(1, steps):
-                relay_far(s, d, False)
-            sided(lambda ds: receive(0, ds), d)
-        new = rim + slab + sum(near[d][1] - near[d][0] for d in far_ds[:piece])
+                for d in far_ds:
+                    relay_far(s, d, False)
+            sided(lambda ds: receive(0, ds), *far_ds)
+        new = planes if far else rim + slab
         for s in range(steps):
             if s:
-                sided(lambda ds: receive(s, ds), *(([0] + near_ds) if piece == 0 else far_ds[piece - 1 : piece]))
+                sided(lambda ds: receive(s, ds), *(far_ds if far else [0] + near_ds))
             march(s, known, new)
-            if piece and s == 0 and piece < len(far_ds):
-                relay_far(0, far_ds[piece], False)
-            if piece == 0 and s == 0:
-                for d in far_ds[1:]:
+            if not far and s == 0:
+                for d in far_ds:
                     relay_far(0, d, True)
                 for later in range(1, steps):
                     for d in far_ds:
                         relay_far(later, d, True)
         known = new
-        if piece == 0:
+        if not far:
             if groups > 1:
                 @pl.when(g != groups - 1)
                 def _():
@@ -564,7 +575,7 @@
 
     count = f32(parts * slab * ny * nz * tiles)
 
-    group = 4 if krylov % 4 == 0 else 1
+    group = 8 if krylov % 8 == 0 else 1
 
     def project(i, carry):
         totals = [jnp.zeros((ny, nz), f32) for _ in range(group)]

time: 23.4 us -> 23.2 us (level)
  no operation moved by 1% of the time
where the time goes in v5:
time: 23.2 us; the launch traced here: 23.1 us
  Pallas kernels  22.4 us (97%)
  between operations  0.67 us (3%)
    pallas_call x1, Pallas kernels, on_device(): pl.pallas_call(functools.partial(kernel, groups, tiles), name='propagate'...  21.7 us
    pallas_call x1, Pallas kernels, scaled(): pl.pallas_call(finish, name='finish', out_shape=tuple((jax.ShapeDtypeStru...  0.72 us

profile of v5, /device:TPU:0, one launch (start us, length us, event | category | flops | bytes accessed | tf_op | source)
XLA Modules:
  0.0 23.1 jit_solution(16915044457034206004)
XLA Ops:
  0.6 21.7 %propagate.1 = (f32[1,5,4,16,128]{4,3,2,1,0:T(8,128)S(1)}, f32[1,32]{1,0:T(1,128)S(1)}, f32[1,128]{1,0:T(1,128)S(1)}, f32[1,128]{1,0:T(1,128)S(1)}) custom-call(f32[5,5]{1,0:T(8,128)} %coupling_in.1, bf16[32,5,4,16,128]{4,3,2,1,0:T(8,128)(2,1)} %basis.1, bf16[1,4,4,16,128]{4,3,2,1,0:T(8,128)(2,1)} %snapshots.1), custom_call_target="tpu_custom_call" | custom-call | tf_op jit(solution)/shard_map/propagate/pallas_call | solution.py:767
  22.4 0.7 %conditional.1 = (f32[1,5,4,16,128]{4,3,2,1,0:T(8,128)}, f32[1,32]{1,0:T(1,128)}, f32[1]{0:T(128)}) conditional(s32[]{:T(128)} %bitcast.2, (f32[1,5,4,16,128]{4,3,2,1,0:T(8,128)S(1)}, f32[1,32]{1,0:T(1,128)S(1)}) %tuple.17, (f32[1,5,4,16,128]{4,3,2,1,0:T(8,128)S(1)}, f32[1,32]{1,0:T(1,128)S(1)}, f32[1,128]{1,0:T(1,128)S(1)}) %tuple.18), branch_computations={%region_0.0_spmd, %region_1.0_spmd} | conditional | bytes 24 | solution.py:844
  22.4 0.7 %finish.3 = (f32[1,5,4,16,128]{4,3,2,1,0:T(8,128)}, f32[1,32]{1,0:T(1,128)}, f32[1,128]{1,0:T(1,128)}) custom-call(f32[1,5,4,16,128]{4,3,2,1,0:T(8,128)S(1)} %get-tuple-element.22.left, f32[1,32]{1,0:T(1,128)S(1)} %get-tuple-element.23.coefs, f32[1,128]{1,0:T(1,128)S(1)} %get-tuple-element.24.square), custom_call_target="tpu_custom_call" | custom-call | tf_op jit(solution)/shard_map/cond/branch_1_fun/finish/pallas_call | solution.py:814

commit v6 on v5

--- a/solution.py
+++ b/solution.py
@@ -77,7 +77,7 @@
             dst[k, pl.ds(p * rows, rows)] = total
         return carry
 
-    unroll = max(n for n in range(1, 5) if planes % n == 0)
+    unroll = max(n for n in range(1, 9) if planes % n == 0)
     lax.fori_loop(0, planes, body, 0, unroll=unroll)
 
 
@@ -456,14 +456,11 @@
             tell(len(levels) + 2, partner(other))
 
     def spread_out(n, send, everyone, reached):
-        way = 2 * (t // max(tiles // 2, 1)) - 1
         others = everyone.at[pl.ds(0, reached * tiles - 1)]
         place = t if reached == 1 else g * tiles + t
 
         def begin():
-            def one(i, carry):
-                peer = lax.rem(2 * tiles - 1 - t + way * i, tiles)
-
+            def one(peer, carry):
                 def to(other):
                     pltpu.make_async_remote_copy(
                         src_ref=send,
@@ -520,7 +517,7 @@
             k = 3 * s + n + 1
             lo, hi = max(k, known - k), new - k
             if hi > lo:
-                first = jnp.where(upper, lo, planes - hi)
+                first = jnp.where(upper, lo, planes - hi) + t // tiles
                 scale = 6.0 ** -steps if k == 3 * steps else 1.0
                 stage(src, state, dst, rates, snap, s, coupling, first, hi - lo, keeps[n], scale)
 
@@ -588,7 +585,7 @@
             rows_k[pl.ds(i * group + n, 1), :] = jnp.sum(totals[n], axis=0, keepdims=True)
         return carry
 
-    lax.fori_loop(0, krylov // group, project, 0)
+    lax.fori_loop(0, krylov // group, project, 0, unroll=2 if krylov % (2 * group) == 0 else 1)
     ones = jnp.ones((8, nz), f32)
     inner = lax.dot_general(
         ones, rows_k[...], (((1,), (1,)), ((), ())), precision=HIGHEST, preferred_element_type=f32
@@ -802,7 +799,7 @@
             dma((2,)),
             dma((groups,)),
             dma((1,)),
-            pltpu.SemaphoreType.REGULAR((tiles.bit_length() + 3 + -(-rim // slab),)),
+            pltpu.SemaphoreType.REGULAR((min(tiles.bit_length() - 1, (-(-rim // slab)).bit_length()) + 4 + -(-rim // slab),)),
         ],
         compiler_params=pltpu.CompilerParams(
             collective_id=0, has_side_effects=True, vmem_limit_bytes=48 << 20

time: 23.2 us -> 22.9 us (0.987)
  Pallas kernels: 22.4 us -> 22 us
    pallas_call x1, Pallas kernels: 21.7 us -> 21.3 us  [on_device(): pl.pallas_call(functools.partial(kernel, groups, tiles), name='propagate'...]
where the time goes in v6:
time: 22.9 us; the launch traced here: 22.7 us
  Pallas kernels  22 us (96%)
  between operations  0.67 us (3%)
    pallas_call x1, Pallas kernels, on_device(): pl.pallas_call(functools.partial(kernel, groups, tiles), name='propagate'...  21.3 us
    pallas_call x1, Pallas kernels, scaled(): pl.pallas_call(finish, name='finish', out_shape=tuple((jax.ShapeDtypeStru...  0.72 us

profile of v6, /device:TPU:0, one launch (start us, length us, event | category | flops | bytes accessed | tf_op | source)
XLA Modules:
  0.0 22.7 jit_solution(7168991703152196347)
XLA Ops:
  0.6 21.3 %propagate.1 = (f32[1,5,4,16,128]{4,3,2,1,0:T(8,128)S(1)}, f32[1,32]{1,0:T(1,128)S(1)}, f32[1,128]{1,0:T(1,128)S(1)}, f32[1,128]{1,0:T(1,128)S(1)}) custom-call(f32[5,5]{1,0:T(8,128)} %coupling_in.1, bf16[32,5,4,16,128]{4,3,2,1,0:T(8,128)(2,1)} %basis.1, bf16[1,4,4,16,128]{4,3,2,1,0:T(8,128)(2,1)} %snapshots.1), custom_call_target="tpu_custom_call" | custom-call | tf_op jit(solution)/shard_map/propagate/pallas_call | solution.py:764
  22.0 0.7 %conditional.1 = (f32[1,5,4,16,128]{4,3,2,1,0:T(8,128)}, f32[1,32]{1,0:T(1,128)}, f32[1]{0:T(128)}) conditional(s32[]{:T(128)} %bitcast.2, (f32[1,5,4,16,128]{4,3,2,1,0:T(8,128)S(1)}, f32[1,32]{1,0:T(1,128)S(1)}) %tuple.17, (f32[1,5,4,16,128]{4,3,2,1,0:T(8,128)S(1)}, f32[1,32]{1,0:T(1,128)S(1)}, f32[1,128]{1,0:T(1,128)S(1)}) %tuple.18), branch_computations={%region_0.0_spmd, %region_1.0_spmd} | conditional | bytes 24 | solution.py:841
  22.0 0.7 %finish.3 = (f32[1,5,4,16,128]{4,3,2,1,0:T(8,128)}, f32[1,32]{1,0:T(1,128)}, f32[1,128]{1,0:T(1,128)}) custom-call(f32[1,5,4,16,128]{4,3,2,1,0:T(8,128)S(1)} %get-tuple-element.22.left, f32[1,32]{1,0:T(1,128)S(1)} %get-tuple-element.23.coefs, f32[1,128]{1,0:T(1,128)S(1)} %get-tuple-element.24.square), custom_call_target="tpu_custom_call" | custom-call | tf_op jit(solution)/shard_map/cond/branch_1_fun/finish/pallas_call | solution.py:811

commit v7 on v6

--- a/solution.py
+++ b/solution.py
@@ -358,7 +358,8 @@
         for s in range(steps):
             send_some(s, False)
 
-    pl.when(t == 0)(send_far)
+    at_end = (t < reach) | (t >= tiles - reach)
+    pl.when(at_end)(send_far)
 
     def flip_step(n):
         if n:
@@ -418,7 +419,7 @@
             piece = lax.dot_general(wide, wide, (((1,), (1,)), ((), ())), preferred_element_type=f32)
             cross[...] = cross[...] + piece if c else piece
             if c == parts // 2:
-                pl.when(t > 0)(send_far)
+                pl.when(jnp.logical_not(at_end))(send_far)
         line = lax.broadcasted_iota(jnp.int32, (size, size), 0)
         column = lax.broadcasted_iota(jnp.int32, (size, size), 1)
         kept = jnp.where(lax.rem(line, ny) == lax.rem(column, ny), cross[...], 0.0)
@@ -439,7 +440,7 @@
         for n in range(len(levels) + 1):
             flip_step(n)
 
-    pl.when((t > 0) & (g != 0))(send_far)
+    pl.when(jnp.logical_not(at_end) & (g != 0))(send_far)
 
     @pl.when(g == groups - 1)
     def _():

time: 22.9 us -> 22.9 us (level)
  no operation moved by 1% of the time
where the time goes in v7:
time: 22.9 us; the launch traced here: 22.7 us
  Pallas kernels  22 us (96%)
  between operations  0.67 us (3%)
    pallas_call x1, Pallas kernels, on_device(): pl.pallas_call(functools.partial(kernel, groups, tiles), name='propagate'...  21.3 us
    pallas_call x1, Pallas kernels, scaled(): pl.pallas_call(finish, name='finish', out_shape=tuple((jax.ShapeDtypeStru...  0.72 us

profile of v7, /device:TPU:0, one launch (start us, length us, event | category | flops | bytes accessed | tf_op | source)
XLA Modules:
  0.0 22.7 jit_solution(5226866953732892682)
XLA Ops:
  0.6 21.3 %propagate.1 = (f32[1,5,4,16,128]{4,3,2,1,0:T(8,128)S(1)}, f32[1,32]{1,0:T(1,128)S(1)}, f32[1,128]{1,0:T(1,128)S(1)}, f32[1,128]{1,0:T(1,128)S(1)}) custom-call(f32[5,5]{1,0:T(8,128)} %coupling_in.1, bf16[32,5,4,16,128]{4,3,2,1,0:T(8,128)(2,1)} %basis.1, bf16[1,4,4,16,128]{4,3,2,1,0:T(8,128)(2,1)} %snapshots.1), custom_call_target="tpu_custom_call" | custom-call | tf_op jit(solution)/shard_map/propagate/pallas_call | solution.py:765
  22.0 0.7 %conditional.1 = (f32[1,5,4,16,128]{4,3,2,1,0:T(8,128)}, f32[1,32]{1,0:T(1,128)}, f32[1]{0:T(128)}) conditional(s32[]{:T(128)} %bitcast.2, (f32[1,5,4,16,128]{4,3,2,1,0:T(8,128)S(1)}, f32[1,32]{1,0:T(1,128)S(1)}) %tuple.17, (f32[1,5,4,16,128]{4,3,2,1,0:T(8,128)S(1)}, f32[1,32]{1,0:T(1,128)S(1)}, f32[1,128]{1,0:T(1,128)S(1)}) %tuple.18), branch_computations={%region_0.0_spmd, %region_1.0_spmd} | conditional | bytes 24 | solution.py:842
  22.0 0.7 %finish.3 = (f32[1,5,4,16,128]{4,3,2,1,0:T(8,128)}, f32[1,32]{1,0:T(1,128)}, f32[1,128]{1,0:T(1,128)}) custom-call(f32[1,5,4,16,128]{4,3,2,1,0:T(8,128)S(1)} %get-tuple-element.22.left, f32[1,32]{1,0:T(1,128)S(1)} %get-tuple-element.23.coefs, f32[1,128]{1,0:T(1,128)S(1)} %get-tuple-element.24.square), custom_call_target="tpu_custom_call" | custom-call | tf_op jit(solution)/shard_map/cond/branch_1_fun/finish/pallas_call | solution.py:812

commit v8 on v7

--- a/solution.py
+++ b/solution.py
@@ -668,6 +668,14 @@
     own_every = jnp.sum(jnp.where(group_row == g, every, 0.0), axis=0, keepdims=True)
     for k in range(krylov):
         spread[k] = jnp.broadcast_to(own_every[:, k : k + 1], (8, nz))
+    for x in range(slab):
+        removed = [jnp.zeros((ny // 8, 8, nz), f32) for _ in range(parts)]
+        for k in range(krylov):
+            factor = spread[k][None]
+            for c in range(parts):
+                removed[c] = removed[c] + factor * plain[k, c, x].reshape(ny // 8, 8, nz)
+        for c in range(parts):
+            left_out[0, c, x] = state[c, pl.ds((rim + x) * ny, ny)] - removed[c].reshape(ny, nz)
     linear = 2.0 * every * first_rows
     bent = every * turned
     bound = jnp.abs(linear) + every * every * reach_row
@@ -678,14 +686,6 @@
     square = jnp.sum(jnp.where(group_row == g, square, 0.0), axis=0, keepdims=True)
     square_out[...] = jnp.broadcast_to(square, square_out.shape)
     coef_out[...] = own_every
-    for x in range(slab):
-        removed = [jnp.zeros((ny // 8, 8, nz), f32) for _ in range(parts)]
-        for k in range(krylov):
-            factor = spread[k][None]
-            for c in range(parts):
-                removed[c] = removed[c] + factor * plain[k, c, x].reshape(ny // 8, 8, nz)
-        for c in range(parts):
-            left_out[0, c, x] = state[c, pl.ds((rim + x) * ny, ny)] - removed[c].reshape(ny, nz)
     coef_drain()
 
 

time: 22.9 us -> 22.9 us (level)
  no operation moved by 1% of the time
where the time goes in v8:
time: 22.9 us; the launch traced here: 22.7 us
  Pallas kernels  22 us (96%)
  between operations  0.67 us (3%)
    pallas_call x1, Pallas kernels, on_device(): pl.pallas_call(functools.partial(kernel, groups, tiles), name='propagate'...  21.3 us
    pallas_call x1, Pallas kernels, scaled(): pl.pallas_call(finish, name='finish', out_shape=tuple((jax.ShapeDtypeStru...  0.72 us

profile of v8, /device:TPU:0, one launch (start us, length us, event | category | flops | bytes accessed | tf_op | source)
XLA Modules:
  0.0 22.7 jit_solution(5226866953732892682)
XLA Ops:
  0.6 21.3 %propagate.1 = (f32[1,5,4,16,128]{4,3,2,1,0:T(8,128)S(1)}, f32[1,32]{1,0:T(1,128)S(1)}, f32[1,128]{1,0:T(1,128)S(1)}, f32[1,128]{1,0:T(1,128)S(1)}) custom-call(f32[5,5]{1,0:T(8,128)} %coupling_in.1, bf16[32,5,4,16,128]{4,3,2,1,0:T(8,128)(2,1)} %basis.1, bf16[1,4,4,16,128]{4,3,2,1,0:T(8,128)(2,1)} %snapshots.1), custom_call_target="tpu_custom_call" | custom-call | tf_op jit(solution)/shard_map/propagate/pallas_call | solution.py:765
  22.0 0.7 %conditional.1 = (f32[1,5,4,16,128]{4,3,2,1,0:T(8,128)}, f32[1,32]{1,0:T(1,128)}, f32[1]{0:T(128)}) conditional(s32[]{:T(128)} %bitcast.2, (f32[1,5,4,16,128]{4,3,2,1,0:T(8,128)S(1)}, f32[1,32]{1,0:T(1,128)S(1)}) %tuple.17, (f32[1,5,4,16,128]{4,3,2,1,0:T(8,128)S(1)}, f32[1,32]{1,0:T(1,128)S(1)}, f32[1,128]{1,0:T(1,128)S(1)}) %tuple.18), branch_computations={%region_0.0_spmd, %region_1.0_spmd} | conditional | bytes 24 | solution.py:842
  22.0 0.7 %finish.3 = (f32[1,5,4,16,128]{4,3,2,1,0:T(8,128)}, f32[1,32]{1,0:T(1,128)}, f32[1,128]{1,0:T(1,128)}) custom-call(f32[1,5,4,16,128]{4,3,2,1,0:T(8,128)S(1)} %get-tuple-element.22.left, f32[1,32]{1,0:T(1,128)S(1)} %get-tuple-element.23.coefs, f32[1,128]{1,0:T(1,128)S(1)} %get-tuple-element.24.square), custom_call_target="tpu_custom_call" | custom-call | tf_op jit(solution)/shard_map/cond/branch_1_fun/finish/pallas_call | solution.py:812
